TPU v7x, 256 devices: a whole 4x4x8 slice. The times are simulated.
256 devices in a mesh: bricks: 4 (over x), grp: 64 (over z, y, core).
Axes of the slice: x: 4, y: 4, z: 8, core: 2. Of those that a mesh axis runs over, the one named last changes fastest.
Arguments:
- features: bfloat16 [2048, 64, 512], P(('bricks', 'grp')), may hold values from -6 to 6
- occupancy: int32 [2048, 512], P(('bricks', 'grp')), may hold values from 0 to 1
- neighbours: int32 [2048, 26], P(('bricks', 'grp')), may hold values from -1 to 2047, as said below
- coarse_map: int32 [2048], P(('bricks', 'grp')), may hold values from 0 to 2047, as said below
- norm_gain: float32 [64], replicated, may hold values from 0.1 to 1.9
- time_shift: float32 [64], replicated, may hold values from -4 to 4
- conv_weight: bfloat16 [27, 64, 64], replicated, may hold values from -0.15625 to 0.15625
- stride_weight: bfloat16 [8, 64, 128], replicated, may hold values from -0.25 to 0.25
- coarse_bias: float32 [128], replicated, may hold values from -3 to 3
Outputs:
- fine_out: bfloat16 [2048, 64, 512], P(('bricks', 'grp'))
- coarse_out: bfloat16 [256, 128, 512], P(('bricks', 'grp'))
Inputs may be any that keep to these rules, and one draw needn't show every extreme that they name: The key orders bricks by x-slab: brick i lies on device i // 8 of bricks+grp, in the slab of cells with x coordinate i // 8. neighbours[i, o] names the brick at offset o from brick i, or -1 where that cell holds no active brick or lies outside the grid. `coarse_map`: every coarse brick has all eight octants, each named once. Coarse brick c is held by device c // 1. Its eight children lie four on device 2 k and four on device 2 k + 1, with k = c // 2; so each device holds the coarse bricks of exactly 4 of its own bricks, and the coarse bricks of its other 4 bricks are held by the device whose index differs in the lowest bit.
All inputs are finite; a program needn't handle non-finite values.
Results may differ from a plain program's by a relative error of at most 0.0047.
Values may be sent and summed in bfloat16 or wider, within the bound.
No kernel may reach another device: no remote copies, remote signals or barrier semaphores. Data moves between devices by JAX's collectives and lax.ppermute only.
A program may use at most 128 MiB of HBM per device.

v0:
```python
import jax
import jax.numpy as jnp
from jax import lax
from jax.sharding import PartitionSpec as P

norm_eps = 1e-06


def padded_2(x, sides, width):
    for axis, dim in sides:
        peers, length = (lax.axis_size(axis), x.shape[dim])
        up = [(i, (i + 1) % peers) for i in range(peers - 1)]
        down = [(j, i) for i, j in up]
        last = lax.slice_in_dim(x, length - width, length, axis=dim)
        initial = lax.slice_in_dim(x, 0, width, axis=dim)
        before = lax.ppermute(last, axis, up)
        after = lax.ppermute(initial, axis, down)
        x = jnp.concatenate([before, x, after], axis=dim)
    return x


def partner(x, axis, bit):
    return lax.ppermute(x, axis, [(i, i ^ 1 << bit) for i in range(lax.axis_size(axis))])


def activate(features, occupancy, norm_gain):
    values = features.astype(jnp.float32)
    scale = lax.rsqrt(jnp.mean(values * values, axis=1, keepdims=True) + norm_eps)
    normed = values * scale * norm_gain[None, :, None]
    mask = occupancy[:, None, :].astype(jnp.float32)
    return (jax.nn.silu(normed) * mask).astype(jnp.bfloat16)


def layer_slice(cubes, axis_pos, shift):
    if shift == -1:
        return lax.slice_in_dim(cubes, 7, 8, axis=axis_pos)
    if shift == 1:
        return lax.slice_in_dim(cubes, 0, 1, axis=axis_pos)
    return cubes


def assemble(center, fetch):
    bricks_here = center.shape[0]
    channels = center.shape[1]
    cube = center.reshape(bricks_here, channels, 8, 8, 8)
    planes = []
    position = 0
    for shift_x in (-1, 0, 1):
        rows_y = []
        for shift_y in (-1, 0, 1):
            cols_z = []
            for shift_z in (-1, 0, 1):
                if shift_x == 0 and shift_y == 0 and (shift_z == 0):
                    cols_z.append(cube)
                else:
                    cols_z.append(fetch(position, shift_x, shift_y, shift_z))
                    position += 1
            rows_y.append(jnp.concatenate(cols_z, axis=4))
        planes.append(jnp.concatenate(rows_y, axis=3))
    return jnp.concatenate(planes, axis=2)


def convolve(padded, conv_weight):
    bricks_here = padded.shape[0]
    channels = padded.shape[1]
    total = jnp.zeros((bricks_here, conv_weight.shape[2], 512), jnp.float32)
    for start_x in range(3):
        for start_y in range(3):
            taps = []
            for start_z in range(3):
                window = padded[
                    :, :, start_x : start_x + 8, start_y : start_y + 8, start_z : start_z + 8
                ]
                taps.append(window.reshape(bricks_here, channels, 512))
            stacked = jnp.concatenate(taps, axis=1)
            first_tap = 9 * start_x + 3 * start_y
            weight = conv_weight[first_tap : first_tap + 3].reshape(3 * channels, -1)
            total = total + jnp.einsum(
                "bcp,cd->bdp", stacked, weight, preferred_element_type=jnp.float32
            )
    return total


def reduce_resolution(fine_features, stride_weight, coarse_bias):
    bricks_here = fine_features.shape[0]
    channels = fine_features.shape[1]
    split = fine_features.reshape(bricks_here, channels, 4, 2, 4, 2, 4, 2)
    kernel = stride_weight.reshape(2, 2, 2, channels, -1)
    octant = jnp.einsum("nciajbkd,abdce->neijk", split, kernel, preferred_element_type=jnp.float32)
    octant = octant + coarse_bias[None, :, None, None, None]
    return octant.reshape(bricks_here, -1).astype(jnp.bfloat16)


def assemble_coarse(placed, coarse_count):
    wide = placed.shape[1] // 64
    shaped = placed.reshape(coarse_count, 2, 2, 2, wide, 4, 4, 4)
    return shaped.transpose(0, 4, 1, 5, 2, 6, 3, 7).reshape(coarse_count, wide, 512)


def shards(
    features,
    occupancy,
    neighbours,
    coarse_map,
    norm_gain,
    time_shift,
    conv_weight,
    stride_weight,
    coarse_bias,
):
    local_count = features.shape[0]
    channels = features.shape[1]
    groups = lax.axis_size("grp")
    device = lax.axis_index("bricks") * groups + lax.axis_index("grp")
    active = activate(features, occupancy, norm_gain)
    cubes = active.reshape(local_count, channels, 8, 8, 8)
    extended = padded_2(active, ((("bricks", "grp"), 0),), local_count)
    lower_face = extended[:local_count].reshape(local_count, channels, 8, 8, 8)[:, :, 7:8]
    upper_face = extended[2 * local_count :].reshape(local_count, channels, 8, 8, 8)[:, :, 0:1]

    def fetch(position, shift_x, shift_y, shift_z):
        target = neighbours[:, position]
        if shift_x == 0:
            source = cubes
            base = device * local_count
        elif shift_x < 0:
            source = lower_face
            base = (device - 1) * local_count
        else:
            source = upper_face
            base = (device + 1) * local_count
        rows = jnp.take(source, jnp.clip(target - base, 0, local_count - 1), axis=0)
        piece = layer_slice(layer_slice(rows, 3, shift_y), 4, shift_z)
        keep = (target >= 0).astype(piece.dtype)
        return piece * keep[:, None, None, None, None]

    padded = assemble(active, fetch)
    conv = convolve(padded, conv_weight)
    summed = features.astype(jnp.float32) + conv + time_shift[None, :, None]
    hidden_state = (occupancy[:, None, :].astype(jnp.float32) * summed).astype(jnp.bfloat16)
    coarse_count = local_count // 8
    half_count = local_count // 2
    coarse_target = coarse_map // 8
    owner_dev = coarse_target // coarse_count
    row_key = coarse_target % coarse_count * 8 + coarse_map % 8
    leaving = (owner_dev != device).astype(jnp.int32)
    order = jnp.argsort(leaving, stable=True)
    stay_rows = order[:half_count]
    go_rows = order[half_count:]
    stay_keys = jnp.take(row_key, stay_rows)
    go_keys = jnp.take(row_key, go_rows)
    sent = jnp.take(hidden_state, go_rows, axis=0)
    arrived, arrived_keys = partner((sent, go_keys), "grp", 0)
    merged_features = jnp.concatenate([jnp.take(hidden_state, stay_rows, axis=0), arrived], axis=0)
    octant_list = reduce_resolution(merged_features, stride_weight, coarse_bias)
    all_keys = jnp.concatenate([stay_keys, arrived_keys], axis=0)
    placed = jnp.zeros_like(octant_list).at[all_keys].set(octant_list)
    return (hidden_state, assemble_coarse(placed, coarse_count))


def solution(mesh):
    return jax.shard_map(
        shards,
        mesh=mesh,
        in_specs=(
            P(("bricks", "grp"), None, None),
            P(("bricks", "grp"), None),
            P(("bricks", "grp"), None),
            P(("bricks", "grp")),
            P(),
            P(),
            P(),
            P(),
            P(),
        ),
        out_specs=(P(("bricks", "grp"), None, None), P(("bricks", "grp"), None, None)),
        check_vma=False,
    )
```

profile of v0, /device:TPU:7, one launch (start us, length us, event | category | flops | bytes accessed | tf_op | source)
XLA Modules:
  0.0 222.2 jit_solution(12427011055042728276)
XLA Ops:
  5.4 3.8 %collective-permute-start = (bf16[8,64,512]{2,1,0:T(8,128)(2,1)}, bf16[8,64,512]{2,1,0:T(8,128)(2,1)}, u32[]{:S(2)}, u32[]{:S(2)}) collective-permute-start(bf16[8,64,512]{2,1,0:T(8,128)(2,1)} %fusion.100), channel_id=1, source_target_pairs={{0,1},{1,2},{2,3},{3,4},{4,5},{5,6},{6,7},{7,8},{8,9},{9,10},{10,1... | collective-permute-start | bytes 1572872 | tf_op jit(solution)/shard_map/ppermute | solution.py:16
  15.3 6.8 %collective-permute-start.2 = (s32[4]{0:T(128)}, s32[4]{0:T(128)}, u32[]{:S(2)}, u32[]{:S(2)}) collective-permute-start(s32[4]{0:T(128)} %broadcast_select_fusion.20), channel_id=1, source_target_pairs={{0,1},{1,0},{2,3},{3,2},{4,5},{5,4},{6,7},{7,6},{8,9},{9,8},{10,11... | collective-permute-start | bytes 56 | tf_op jit(solution)/shard_map/ppermute | solution.py:23
  59.5 2.6 %pad_maximum_fusion.1 = (bf16[8,64,8,8,8]{1,4,3,2,0:T(8,128)(2,1)}, bf16[8,64,8,8,8]{1,4,3,2,0:T(8,128)(2,1)}) fusion(bf16[8,64,8,8,8]{1,4,3,2,0:T(8,128)(2,1)S(1)} %bitcast.283, bf16[8,64,8,8,1]{1,4,3,2,0:T(2,128)(2,1)S(1)} %fusion.104, bf16[8,64,8,8,1]{1,4,3,2,0:T(2,128)(2,1)S(1)} %fusion.105), kind=kLoop, calls=%fused_computation.114 | loop fusion | flops 2097152 | bytes 1703936 | tf_op jit(solution)/shard_map/concatenate | solution.py:58
  68.3 3.6 %maximum_maximum_fusion.3 = (bf16[8,64,8,9,10]{1,4,3,2,0:T(8,128)(2,1)S(1)}, bf16[8,64,8,9,10]{1,4,3,2,0:T(8,128)(2,1)S(1)}) fusion(bf16[8,64,8,1,1]{1,4,3,2,0:T(2,128)(2,1)S(1)} %fusion.118, bf16[8,64,8,1,8]{1,4,3,2,0:T(8,128)(2,1)S(1)} %fusion.107, bf16[8,64,8,1,1]{1,4,3,2,0:T(2,128)(2,1)S(1)} %fusion.117, bf16[8,64,8,8,1]{1,4,3,2,0:T(2,128)(2,1)S(1)} %fusion.105, ...), kind=kLoop, calls=%fused_computation.34 | loop fusion | flops 8847360 | bytes 2293760 | tf_op jit(solution)/shard_map/concatenate | solution.py:59
  74.0 2.4 %copy.151 = bf16[8,64,512]{2,1,0:T(8,128)(2,1)} copy(bf16[8,64,512]{1,2,0:T(8,128)(2,1)} %bitcast.329) | data formatting | bytes 1048576 | tf_op jit(solution)/shard_map/reshape | solution.py:74
  83.4 2.4 %copy.153 = bf16[8,64,512]{2,1,0:T(8,128)(2,1)} copy(bf16[8,64,512]{1,2,0:T(8,128)(2,1)} %bitcast.305) | data formatting | bytes 1048576 | tf_op jit(solution)/shard_map/reshape | solution.py:74
  87.9 2.5 %copy.158 = bf16[8,64,512]{2,1,0:T(8,128)(2,1)} copy(bf16[8,64,512]{1,2,0:T(8,128)(2,1)} %bitcast.330) | data formatting | bytes 1048576 | tf_op jit(solution)/shard_map/reshape | solution.py:74
  90.4 2.4 %copy.157 = bf16[8,64,512]{2,1,0:T(8,128)(2,1)} copy(bf16[8,64,512]{1,2,0:T(8,128)(2,1)} %bitcast.328) | data formatting | bytes 1048576 | tf_op jit(solution)/shard_map/reshape | solution.py:74
  116.3 3.4 %maximum_maximum_fusion = bf16[8,64,9,10,10]{1,4,3,2,0:T(8,128)(2,1)S(1)} fusion(bf16[8,64,8,1,1]{1,4,3,2,0:T(2,128)(2,1)S(1)} %copy-done.13, bf16[8,64,8,1,8]{1,4,3,2,0:T(8,128)(2,1)S(1)} %copy-done.8, bf16[8,64,8,1,1]{1,4,3,2,0:T(2,128)(2,1)S(1)} %copy-done.15, bf16[8,64,8,8,1]{1,4,3,2,0:T(2,128)(2,1)S(1)} %copy-done.2, ...), kind=kLoop, calls=%fused_computation.31 | loop fusion | flops 9216000 | bytes 1843200 | tf_op jit(solution)/shard_map/concatenate | solution.py:60
  119.7 3.9 %fusion.170 = (bf16[8,64,8,8,8]{1,4,3,2,0:T(8,128)(2,1)S(1)}, bf16[8,64,8,8,8]{1,4,3,2,0:T(8,128)(2,1)}, bf16[8,64,8,8,8]{1,4,3,2,0:T(8,128)(2,1)}, bf16[8,64,8,...) fusion(bf16[8,64,9,10,10]{1,4,3,2,0:T(8,128)(2,1)S(1)} %maximum, ...), kind=kLoop, calls=%fused_computation.337 | loop fusion | bytes 9437184 | tf_op jit(solution)/shard_map/slice | solution.py:71
  123.6 2.4 %copy.139 = bf16[8,64,512]{2,1,0:T(8,128)(2,1)} copy(bf16[8,64,512]{1,2,0:T(8,128)(2,1)} %bitcast.323) | data formatting | bytes 1048576 | tf_op jit(solution)/shard_map/reshape | solution.py:74
  125.9 2.4 %copy.138 = bf16[8,64,512]{2,1,0:T(8,128)(2,1)} copy(bf16[8,64,512]{1,2,0:T(8,128)(2,1)} %bitcast.321) | data formatting | bytes 1048576 | tf_op jit(solution)/shard_map/reshape | solution.py:74
  128.3 2.4 %copy.137 = bf16[8,64,512]{2,1,0:T(8,128)(2,1)} copy(bf16[8,64,512]{1,2,0:T(8,128)(2,1)} %bitcast.319) | data formatting | bytes 1048576 | tf_op jit(solution)/shard_map/reshape | solution.py:74
  130.7 2.4 %copy.143 = bf16[8,64,512]{2,1,0:T(8,128)(2,1)} copy(bf16[8,64,512]{1,2,0:T(8,128)(2,1)} %bitcast.317) | data formatting | bytes 1048576 | tf_op jit(solution)/shard_map/reshape | solution.py:74
  133.1 2.4 %copy.142 = bf16[8,64,512]{2,1,0:T(8,128)(2,1)} copy(bf16[8,64,512]{1,2,0:T(8,128)(2,1)} %bitcast.315) | data formatting | bytes 1048576 | tf_op jit(solution)/shard_map/reshape | solution.py:74
  135.4 2.3 %copy.141 = bf16[8,64,512]{2,1,0:T(8,128)(2,1)} copy(bf16[8,64,512]{1,2,0:T(8,128)(2,1)} %bitcast.313) | data formatting | bytes 1048576 | tf_op jit(solution)/shard_map/reshape | solution.py:74
  137.8 2.4 %copy.147 = bf16[8,64,512]{2,1,0:T(8,128)(2,1)} copy(bf16[8,64,512]{1,2,0:T(8,128)(2,1)} %bitcast.311) | data formatting | bytes 1048576 | tf_op jit(solution)/shard_map/reshape | solution.py:74
  158.2 7.3 %maximum_maximum_fusion.1 = bf16[8,64,9,10,10]{1,4,3,2,0:T(8,128)(2,1)S(1)} fusion(bf16[8,64,1,1,1]{1,4,3,2,0:T(2,128)(2,1)S(1)} %fusion.132, bf16[8,64,1,1,8]{1,4,3,2,0:T(8,128)(2,1)S(1)} %fusion.121, bf16[8,64,1,1,1]{1,4,3,2,0:T(2,128)(2,1)S(1)} %fusion.131, bf16[8,64,1,8,1]{1,4,3,2,0:T(2,128)(2,1)S(1)} %fusion.120, ...), kind=kLoop, calls=%fused_computation.32 | loop fusion | flops 16588800 | bytes 1843200 | tf_op jit(solution)/shard_map/concatenate | solution.py:60
  165.5 3.5 %fusion.169 = (bf16[8,64,8,8,8]{1,4,3,2,0:T(8,128)(2,1)S(1)}, bf16[8,64,8,8,8]{1,4,3,2,0:T(8,128)(2,1)S(1)}, bf16[8,64,8,8,8]{1,4,3,2,0:T(8,128)(2,1)S(1)}, bf16...) fusion(bf16[8,64,9,10,10]{1,4,3,2,0:T(8,128)(2,1)S(1)} %maximum, ...), kind=kLoop, calls=%fused_computation.336 | loop fusion | bytes 9437184 | tf_op jit(solution)/shard_map/slice | solution.py:71
  169.0 2.3 %copy.172 = bf16[8,64,512]{2,1,0:T(8,128)(2,1)} copy(bf16[8,64,512]{1,2,0:T(8,128)(2,1)} %bitcast.324) | data formatting | bytes 1048576 | tf_op jit(solution)/shard_map/reshape | solution.py:74
  173.7 2.4 %copy.170 = bf16[8,64,512]{2,1,0:T(8,128)(2,1)} copy(bf16[8,64,512]{1,2,0:T(8,128)(2,1)} %bitcast.320) | data formatting | bytes 1048576 | tf_op jit(solution)/shard_map/reshape | solution.py:74
  176.1 2.3 %copy.176 = bf16[8,64,512]{2,1,0:T(8,128)(2,1)} copy(bf16[8,64,512]{1,2,0:T(8,128)(2,1)} %bitcast.318) | data formatting | bytes 1048576 | tf_op jit(solution)/shard_map/reshape | solution.py:74
  204.3 11.0 %reshape.739 = bf16[1,2,2,2,128,4,4,4]{7,6,5,4,3,2,1,0:T(4,128)(2,1)} reshape(bf16[8,8192]{1,0:T(8,128)(2,1)S(1)} %scatter_custom_fusion) | data formatting | bytes 262144 | tf_op jit(solution)/shard_map/reshape | solution.py:96
  215.3 6.1 %copy.186 = bf16[1,128,2,4,2,4,2,4]{1,7,6,5,4,3,2,0:T(4,128)(2,1)S(1)} copy(bf16[1,128,2,4,2,4,2,4]{7,5,3,1,6,4,2,0:T(4,128)(2,1)} %bitcast.287) | data formatting | bytes 262144 | tf_op jit(solution)/shard_map/transpose | solution.py:97
  (348 shorter events, 135.0 us)
Async XLA Ops:
  0.6 199.5 %copy-start = (bf16[8,64,128]{2,1,0:T(8,128)(2,1)S(1)}, bf16[8,64,128]{2,1,0:T(8,128)(2,1)}, u32[]{:S(2)}) copy-start(bf16[8,64,128]{2,1,0:T(8,128)(2,1)} %param.24) | copy-start | bytes 393220
  0.6 23.0 %copy-start.6 = (s32[8,26]{1,0:T(8,128)S(1)}, s32[8,26]{1,0:T(8,128)}, u32[]{:S(2)}) copy-start(s32[8,26]{1,0:T(8,128)} %param.19) | copy-start | bytes 2500
  5.4 95.7 %collective-permute-start = (bf16[8,64,512]{2,1,0:T(8,128)(2,1)}, bf16[8,64,512]{2,1,0:T(8,128)(2,1)}, u32[]{:S(2)}, u32[]{:S(2)}) collective-permute-start(bf16[8,64,512]{2,1,0:T(8,128)(2,1)} %fusion.100), channel_id=1, source_target_pairs={{0,1},{1,2},{2,3},{3,4},{4,5},{5,6},{6,7},{7,8},{8,9},{9,10},{10,1... | collective-permute-start | bytes 1572872 | tf_op jit(solution)/shard_map/ppermute | solution.py:16
  9.2 134.4 %collective-permute-start.1 = (bf16[8,64,512]{2,1,0:T(8,128)(2,1)}, bf16[8,64,512]{2,1,0:T(8,128)(2,1)}, u32[]{:S(2)}, u32[]{:S(2)}) collective-permute-start(bf16[8,64,512]{2,1,0:T(8,128)(2,1)} %fusion.100), channel_id=1, source_target_pairs={{1,0},{2,1},{3,2},{4,3},{5,4},{6,5},{7,6},{8,7},{9,8},{10,9},{11,1... | collective-permute-start | bytes 1572872 | tf_op jit(solution)/shard_map/ppermute | solution.py:17
  15.3 182.4 %collective-permute-start.2 = (s32[4]{0:T(128)}, s32[4]{0:T(128)}, u32[]{:S(2)}, u32[]{:S(2)}) collective-permute-start(s32[4]{0:T(128)} %broadcast_select_fusion.20), channel_id=1, source_target_pairs={{0,1},{1,0},{2,3},{3,2},{4,5},{5,4},{6,7},{7,6},{8,9},{9,8},{10,11... | collective-permute-start | bytes 56 | tf_op jit(solution)/shard_map/ppermute | solution.py:23
  59.0 12.9 %copy-start.1 = (bf16[8,64,8,8,1]{1,4,3,2,0:T(2,128)(2,1)}, bf16[8,64,8,8,1]{1,4,3,2,0:T(2,128)(2,1)S(1)}, u32[]{:S(2)}) copy-start(bf16[8,64,8,8,1]{1,4,3,2,0:T(2,128)(2,1)S(1)} %fusion.105) | copy-start | bytes 196612
  59.5 12.4 %copy-start.3 = (bf16[8,64,8,8,1]{1,4,3,2,0:T(2,128)(2,1)}, bf16[8,64,8,8,1]{1,4,3,2,0:T(2,128)(2,1)S(1)}, u32[]{:S(2)}) copy-start(bf16[8,64,8,8,1]{1,4,3,2,0:T(2,128)(2,1)S(1)} %fusion.104) | copy-start | bytes 196612
  63.1 8.9 %copy-start.12 = (bf16[8,64,8,1,1]{1,4,3,2,0:T(2,128)(2,1)}, bf16[8,64,8,1,1]{1,4,3,2,0:T(2,128)(2,1)S(1)}, u32[]{:S(2)}) copy-start(bf16[8,64,8,1,1]{1,4,3,2,0:T(2,128)(2,1)S(1)} %fusion.118) | copy-start | bytes 24580
  87.8 8.5 %copy-start.61 = (s32[8]{0:T(128)S(1)}, s32[8]{0:T(128)}, u32[]{:S(2)}) copy-start(s32[8]{0:T(128)} %get-tuple-element.25) | copy-start | bytes 100
  87.8 9.1 %copy-start.60 = (s32[8]{0:T(128)S(1)}, s32[8]{0:T(128)}, u32[]{:S(2)}) copy-start(s32[8]{0:T(128)} %get-tuple-element.154) | copy-start | bytes 100
  87.8 9.6 %copy-start.63 = (s32[8]{0:T(128)S(1)}, s32[8]{0:T(128)}, u32[]{:S(2)}) copy-start(s32[8]{0:T(128)} %get-tuple-element.21) | copy-start | bytes 100
  87.8 10.2 %copy-start.62 = (s32[8]{0:T(128)S(1)}, s32[8]{0:T(128)}, u32[]{:S(2)}) copy-start(s32[8]{0:T(128)} %get-tuple-element.156) | copy-start | bytes 100
  87.8 10.8 %copy-start.64 = (s32[4]{0:T(128)S(1)}, s32[4]{0:T(128)}, u32[]{:S(2)}) copy-start(s32[4]{0:T(128)} %get-tuple-element.13) | copy-start | bytes 52
  87.8 11.5 %copy-start.65 = (s32[8]{0:T(128)S(1)}, s32[8]{0:T(128)}, u32[]{:S(2)}) copy-start(s32[8]{0:T(128)} %get-tuple-element.17) | copy-start | bytes 100
  87.8 12.6 %copy-start.46 = (bf16[27,64,64]{2,1,0:T(8,128)(2,1)S(1)}, bf16[27,64,64]{2,1,0:T(8,128)(2,1)}, u32[]{:S(2)}) copy-start(bf16[27,64,64]{2,1,0:T(8,128)(2,1)} %param.23) | copy-start | bytes 663556
  107.6 8.5 %copy-start.2 = (bf16[8,64,8,8,1]{1,4,3,2,0:T(2,128)(2,1)S(1)}, bf16[8,64,8,8,1]{1,4,3,2,0:T(2,128)(2,1)}, u32[]{:S(2)}) copy-start(bf16[8,64,8,8,1]{1,4,3,2,0:T(2,128)(2,1)} %copy-done.1) | copy-start | bytes 196612
  107.6 8.5 %copy-start.4 = (bf16[8,64,8,8,1]{1,4,3,2,0:T(2,128)(2,1)S(1)}, bf16[8,64,8,8,1]{1,4,3,2,0:T(2,128)(2,1)}, u32[]{:S(2)}) copy-start(bf16[8,64,8,8,1]{1,4,3,2,0:T(2,128)(2,1)} %copy-done.3) | copy-start | bytes 196612
  107.7 8.5 %copy-start.8 = (bf16[8,64,8,1,8]{1,4,3,2,0:T(8,128)(2,1)S(1)}, bf16[8,64,8,1,8]{1,4,3,2,0:T(8,128)(2,1)}, u32[]{:S(2)}) copy-start(bf16[8,64,8,1,8]{1,4,3,2,0:T(8,128)(2,1)} %copy-done.7) | copy-start | bytes 196612
  107.7 8.5 %copy-start.10 = (bf16[8,64,8,1,8]{1,4,3,2,0:T(8,128)(2,1)S(1)}, bf16[8,64,8,1,8]{1,4,3,2,0:T(8,128)(2,1)}, u32[]{:S(2)}) copy-start(bf16[8,64,8,1,8]{1,4,3,2,0:T(8,128)(2,1)} %copy-done.9) | copy-start | bytes 196612
  107.7 8.5 %copy-start.13 = (bf16[8,64,8,1,1]{1,4,3,2,0:T(2,128)(2,1)S(1)}, bf16[8,64,8,1,1]{1,4,3,2,0:T(2,128)(2,1)}, u32[]{:S(2)}) copy-start(bf16[8,64,8,1,1]{1,4,3,2,0:T(2,128)(2,1)} %copy-done.12) | copy-start | bytes 24580
  107.7 8.5 %copy-start.15 = (bf16[8,64,8,1,1]{1,4,3,2,0:T(2,128)(2,1)S(1)}, bf16[8,64,8,1,1]{1,4,3,2,0:T(2,128)(2,1)}, u32[]{:S(2)}) copy-start(bf16[8,64,8,1,1]{1,4,3,2,0:T(2,128)(2,1)} %copy-done.14) | copy-start | bytes 24580
  107.7 8.5 %copy-start.17 = (bf16[8,64,8,1,1]{1,4,3,2,0:T(2,128)(2,1)S(1)}, bf16[8,64,8,1,1]{1,4,3,2,0:T(2,128)(2,1)}, u32[]{:S(2)}) copy-start(bf16[8,64,8,1,1]{1,4,3,2,0:T(2,128)(2,1)} %copy-done.16) | copy-start | bytes 24580
  107.7 8.5 %copy-start.19 = (bf16[8,64,8,1,1]{1,4,3,2,0:T(2,128)(2,1)S(1)}, bf16[8,64,8,1,1]{1,4,3,2,0:T(2,128)(2,1)}, u32[]{:S(2)}) copy-start(bf16[8,64,8,1,1]{1,4,3,2,0:T(2,128)(2,1)} %copy-done.18) | copy-start | bytes 24580
  197.6 1.6 collective-permute-start.3
  (49 other events, 117.9 us)
where the time goes:
time: 224 us; the launch traced here: 222 us
  local copies, waits for them, and re-layouts  128 us (57%)
  other arithmetic  72.9 us (33%)
  starting transfers between devices  12.6 us (6%)
  matrix products  6.84 us (3%)
    reshape x26, local copies, waits for them, and re-layouts, convolve(): taps.append(window.reshape(bricks_here, channels, 512))  55.3 us
    gather x26, local copies, waits for them, and re-layouts, fetch(): rows = jnp.take(source, jnp.clip(target - base, 0, local_count - 1), axis=0)  24.2 us
    mul x26, other arithmetic, fetch(): return piece * keep[:, None, None, None, None]  20.2 us
    slice x4, local copies, waits for them, and re-layouts, convolve(): padded[:, :, start_x:start_x + 8, start_y:start_y + 8, start_z:start_z + 8]  11.4 us
    reshape x1, local copies, waits for them, and re-layouts, assemble_coarse(): shaped = placed.reshape(coarse_count, 2, 2, 2, wide, 4, 4, 4)  11 us
    gather x28, other arithmetic  10.7 us
    concatenate x2, other arithmetic, assemble(): return jnp.concatenate(planes, axis=2)  10.7 us
    convert_element_type x26, other arithmetic, fetch(): keep = (target >= 0).astype(piece.dtype)  9.82 us
  transfers between devices with their start and end apart: 4, of which 0 were waited for; matrix products, arithmetic and copies ran while one was open for 79% of the time, Pallas kernels for 0%

commit v1 on v0

v1 whole, which is shorter than its diff:
```python
import jax
import jax.numpy as jnp
from jax import lax
from jax.experimental import pallas as pl
from jax.experimental.pallas import tpu as pltpu
from jax.sharding import PartitionSpec as P

BF = jnp.bfloat16
F32 = jnp.float32
EPS = 1e-06
BRK = 8
CH = 64
CH2 = 128
VOX = 512
LANES = 128
TAPS = 9

ROLLS = (0, 64, 8, 120, 72, 56)
PLAIN, SWAP, UP, DOWN, SWAP_UP, SWAP_DOWN = range(6)


def column(row):
    n = row.shape[1]
    wide = jnp.broadcast_to(row, (n, n))
    on = lax.broadcasted_iota(jnp.int32, (n, n), 0) == lax.broadcasted_iota(jnp.int32, (n, n), 1)
    return jnp.sum(jnp.where(on, wide, 0.0), axis=1, keepdims=True)


def activate(x, occupied, gain):
    scale = lax.rsqrt(jnp.mean(x * x, axis=0, keepdims=True) + EPS)
    normed = x * scale * gain
    return (normed * jax.nn.sigmoid(normed) * occupied).astype(BF)


def position(dx, dy, dz):
    place = 9 * (dx + 1) + 3 * (dy + 1) + (dz + 1)
    return place - 1 if place > 13 else place


def slot(nb_ref, brick, dx, dy, dz):
    target = nb_ref[brick, position(dx, dy, dz)]
    return jnp.where(target < 0, BRK, target & (BRK - 1))


def lane_masks():
    lane = lax.broadcasted_iota(jnp.int32, (CH, LANES), 1)
    z = lane & 7
    y = (lane >> 3) & 7
    return z == 0, z == 7, y == 0, y == 7, lane < 64


def shifted(take, masks):
    z0, z7, y0, y7, _ = masks
    centre = take(PLAIN, 0, 0)
    edge = jnp.where(y0, take(SWAP, 1, 0), take(SWAP, -1, 0))
    edge_up = jnp.where(y0, take(SWAP_UP, -1, 1), take(SWAP_UP, 1, 1))
    edge_down = jnp.where(y7, take(SWAP_DOWN, 1, -1), take(SWAP_DOWN, -1, -1))
    middle = {
        -1: pltpu.roll(jnp.where(z7, take(DOWN, 0, -1), centre), 1, 1),
        0: centre,
        1: pltpu.roll(jnp.where(z0, take(UP, 0, 1), centre), 127, 1),
    }
    edges = {
        -1: pltpu.roll(jnp.where(z7, edge_down, edge), 1, 1),
        0: edge,
        1: pltpu.roll(jnp.where(z0, edge_up, edge), 127, 1),
    }
    out = []
    for b in (-1, 0, 1):
        for c in (-1, 0, 1):
            if b == -1:
                out.append(pltpu.roll(jnp.where(y7, edges[c], middle[c]), 8, 1))
            elif b == 0:
                out.append(middle[c])
            else:
                out.append(pltpu.roll(jnp.where(y0, edges[c], middle[c]), 120, 1))
    return out


def faces_kernel(low_ref, high_ref, occ_low_ref, occ_high_ref, gain_ref, down_ref, up_ref):
    gain = column(gain_ref[...])
    for source, occ, target in ((low_ref, occ_low_ref, down_ref), (high_ref, occ_high_ref, up_ref)):
        for i in range(BRK):
            occupied = occ[i : i + 1, :].astype(F32)
            target[i] = activate(source[i].astype(F32), occupied, gain)


def inner_kernel(
    nb_ref, features_ref, occ_ref, gain_ref, shift_ref, weight_ref, base_ref, acts, wide, stack
):
    gain = column(gain_ref[...])
    shift = column(shift_ref[...])
    masks = lane_masks()
    low = lax.broadcasted_iota(jnp.int32, (CH, LANES), 1) < 64
    for kind in range(len(ROLLS)):
        acts[kind, BRK] = jnp.zeros((CH, VOX), BF)
    for i in range(BRK):
        occupied = occ_ref[i : i + 1, :].astype(F32)
        active = activate(features_ref[i].astype(F32), occupied, gain)
        acts[PLAIN, i] = active
        for j in range(4):
            cols = slice(j * LANES, (j + 1) * LANES)
            for kind in range(1, len(ROLLS)):
                acts[kind, i, :, cols] = pltpu.roll(active[:, cols], ROLLS[kind], 1)
    for a in range(3):
        wide[a * CH : (a + 1) * CH, :] = (
            weight_ref[TAPS * a : TAPS * (a + 1)].reshape(TAPS * CH, CH).T
        )
    for i in range(BRK):
        slots = {
            (dy, dz): i if (dy, dz) == (0, 0) else slot(nb_ref, i, 0, dy, dz)
            for dy in (-1, 0, 1)
            for dz in (-1, 0, 1)
        }
        for j in range(4):
            cols = slice(j * LANES, (j + 1) * LANES)
            pieces = shifted(lambda kind, dy, dz: acts[kind, slots[dy, dz], :, cols], masks)
            for tap, piece in enumerate(pieces):
                stack[i % 2, tap * CH : (tap + 1) * CH, cols] = piece
        y = jnp.dot(wide[...], stack[i % 2], preferred_element_type=F32)
        for j in range(4):
            cols = slice(j * LANES, (j + 1) * LANES)
            before = slice((j - 1) * LANES, j * LANES)
            after = slice((j + 1) * LANES, (j + 2) * LANES)
            to_high = y[2 * CH :, cols]
            if j > 0:
                to_high = to_high + y[:CH, before]
            to_low = y[:CH, cols]
            if j < 3:
                to_low = to_low + y[2 * CH :, after]
            moved = pltpu.roll(jnp.where(low, to_low, to_high), 64, 1)
            total = y[CH : 2 * CH, cols] + moved + features_ref[i, :, cols].astype(F32) + shift
            base_ref[i, :, cols] = total


def outer_kernel(
    nb_ref,
    map_ref,
    dev_ref,
    base_ref,
    up_ref,
    down_ref,
    occ_ref,
    weight_ref,
    stride_ref,
    bias_ref,
    fine_ref,
    stay_ref,
    leave_ref,
    halo,
    wide,
    wide2,
    stack,
    picked,
    placing,
):
    masks = lane_masks()
    low = masks[4]
    low32 = lax.broadcasted_iota(jnp.int32, (CH, LANES), 1) < 64
    for side, source in ((0, down_ref), (1, up_ref)):
        for kind, roll in enumerate(ROLLS):
            halo[side, kind, BRK] = jnp.zeros((CH, LANES), BF)
            for i in range(BRK):
                face = source[i]
                halo[side, kind, i] = pltpu.roll(face, roll, 1) if roll else face
    for row, a in enumerate((0, 2)):
        wide[row * CH : (row + 1) * CH, :] = (
            weight_ref[TAPS * a : TAPS * (a + 1)].reshape(TAPS * CH, CH).T
        )
    wide2[...] = stride_ref[...].reshape(8 * CH, CH2).T
    for i in range(BRK):

        def take(kind, dy, dz):
            beyond = halo[0, kind, slot(nb_ref, i, 1, dy, dz)]
            ahead = halo[1, kind, slot(nb_ref, i, -1, dy, dz)]
            if kind in (SWAP, SWAP_UP, SWAP_DOWN):
                first, second = ahead, beyond
            else:
                first, second = beyond, ahead
            if kind in (UP, SWAP_UP):
                return first, second
            return first, second

        def merged(kind, dy, dz):
            first, second = take(kind, dy, dz)
            return jnp.where(split[kind], first, second)

        lane = lax.broadcasted_iota(jnp.int32, (CH, LANES), 1)
        split = {}
        for kind, roll in enumerate(ROLLS):
            moved = 8 if kind in (UP, SWAP_UP) else (-8 if kind in (DOWN, SWAP_DOWN) else 0)
            split[kind] = ((lane - moved) & 127) < 64
        pieces = shifted(merged, masks)
        for tap, piece in enumerate(pieces):
            stack[tap * CH : (tap + 1) * CH, i * LANES : (i + 1) * LANES] = piece
    edge = jnp.dot(wide[...], stack[...], preferred_element_type=F32)
    for i in range(BRK):
        cols = slice(i * LANES, (i + 1) * LANES)
        moved = pltpu.roll(jnp.where(low32, edge[CH:, cols], edge[:CH, cols]), 64, 1)
        for j in range(4):
            cols = slice(j * LANES, (j + 1) * LANES)
            total = base_ref[i, :, cols]
            if j == 0:
                total = total + jnp.where(low32, moved, 0.0)
            if j == 3:
                total = total + jnp.where(low32, 0.0, moved)
            fine = (occ_ref[i : i + 1, cols].astype(F32) * total).astype(BF)
            fine_ref[i, :, cols] = fine

    source = lax.broadcasted_iota(jnp.int32, (VOX, VOX), 0)
    lane = lax.broadcasted_iota(jnp.int32, (VOX, VOX), 1)
    tap = lane >> 6
    wanted = (
        (2 * ((lane >> 4) & 3) + ((tap >> 2) & 1)) * 64
        + (2 * ((lane >> 2) & 3) + ((tap >> 1) & 1)) * 8
        + 2 * (lane & 3)
        + (tap & 1)
    )
    select = (source == wanted).astype(BF)
    for pair in range(BRK // 2):
        both = fine_ref[2 * pair : 2 * pair + 2].reshape(2 * CH, VOX)
        sorted_ = jnp.dot(both, select, preferred_element_type=F32).astype(BF)
        first, second = sorted_[:CH], sorted_[CH:]
        for j in range(4):
            cols = slice(j * LANES, (j + 1) * LANES)
            one, two = first[:, cols], second[:, cols]
            target = slice(pair * LANES, (pair + 1) * LANES)
            picked[2 * j * CH : (2 * j + 1) * CH, target] = jnp.where(
                low, one, pltpu.roll(two, 64, 1)
            )
            picked[(2 * j + 1) * CH : (2 * j + 2) * CH, target] = jnp.where(
                low, pltpu.roll(one, 64, 1), two
            )
    octant = jnp.dot(wide2[...], picked[...], preferred_element_type=F32)
    octant = (octant + column(bias_ref[...])).astype(BF)

    entry = lax.broadcasted_iota(jnp.int32, (CH, VOX), 0)
    voxel = lax.broadcasted_iota(jnp.int32, (CH, VOX), 1)
    from_entry = ((voxel >> 6) & 3) * 16 + ((voxel >> 3) & 3) * 4 + (voxel & 3)
    of_octant = ((voxel >> 8) & 1) * 4 + ((voxel >> 5) & 1) * 2 + ((voxel >> 2) & 1)
    hit = jnp.where(entry == from_entry, of_octant, -1)
    for i in range(BRK):
        target = map_ref[i]
        stays = (target >> 3) == dev_ref[0]
        which = target & 7
        rows = slice(i * CH, (i + 1) * CH)
        placing[rows, :VOX] = (hit == jnp.where(stays, which, 8)).astype(BF)
        placing[rows, VOX:] = (hit == jnp.where(stays, 8, which)).astype(BF)
    placed = jnp.dot(octant, placing[...], preferred_element_type=F32).astype(BF)
    stay_ref[...] = placed[:, :VOX]
    leave_ref[...] = placed[:, VOX:]


def shards(
    features,
    occupancy,
    neighbours,
    coarse_map,
    norm_gain,
    time_shift,
    conv_weight,
    stride_weight,
    coarse_bias,
):
    groups = lax.axis_size("grp")
    total = lax.axis_size("bricks") * groups
    device = lax.axis_index("bricks") * groups + lax.axis_index("grp")
    vmem = pl.BlockSpec(memory_space=pltpu.VMEM)
    smem = pl.BlockSpec(memory_space=pltpu.SMEM)
    gain = norm_gain.reshape(1, CH)
    shift = time_shift.reshape(1, CH)
    bias = coarse_bias.reshape(1, CH2)

    faces = jax.ShapeDtypeStruct((BRK, CH, LANES), BF)
    down, up = pl.pallas_call(
        faces_kernel,
        grid=(1,),
        in_specs=[
            pl.BlockSpec((BRK, CH, LANES), lambda i: (0, 0, 0)),
            pl.BlockSpec((BRK, CH, LANES), lambda i: (0, 0, 3)),
            pl.BlockSpec((BRK, LANES), lambda i: (0, 0)),
            pl.BlockSpec((BRK, LANES), lambda i: (0, 3)),
            pl.BlockSpec((1, CH), lambda i: (0, 0)),
        ],
        out_specs=[pl.BlockSpec((BRK, CH, LANES), lambda i: (0, 0, 0))] * 2,
        out_shape=(faces, faces),
        name="faces",
    )(features, features, occupancy, occupancy, gain)

    pairs = [(i, i + 1) for i in range(total - 1)]
    from_below = lax.ppermute(up, ("bricks", "grp"), pairs)
    from_above = lax.ppermute(down, ("bricks", "grp"), [(j, i) for i, j in pairs])

    base = pl.pallas_call(
        inner_kernel,
        in_specs=[smem, vmem, vmem, vmem, vmem, vmem],
        out_specs=vmem,
        out_shape=jax.ShapeDtypeStruct((BRK, CH, VOX), F32),
        scratch_shapes=[
            pltpu.VMEM((len(ROLLS), BRK + 1, CH, VOX), BF),
            pltpu.VMEM((3 * CH, TAPS * CH), BF),
            pltpu.VMEM((2, TAPS * CH, VOX), BF),
        ],
        compiler_params=pltpu.CompilerParams(vmem_limit_bytes=24 << 20),
        cost_estimate=pl.CostEstimate(
            flops=2 * 27 * CH * CH * VOX * BRK, bytes_accessed=2 << 20, transcendentals=0
        ),
        name="inner",
    )(neighbours, features, occupancy, gain, shift, conv_weight)

    fine, stay, leave = pl.pallas_call(
        outer_kernel,
        in_specs=[smem, smem, smem] + [vmem] * 7,
        out_specs=[vmem] * 3,
        out_shape=(
            jax.ShapeDtypeStruct((BRK, CH, VOX), BF),
            jax.ShapeDtypeStruct((CH2, VOX), BF),
            jax.ShapeDtypeStruct((CH2, VOX), BF),
        ),
        scratch_shapes=[
            pltpu.VMEM((2, len(ROLLS), BRK + 1, CH, LANES), BF),
            pltpu.VMEM((2 * CH, TAPS * CH), BF),
            pltpu.VMEM((CH2, 8 * CH), BF),
            pltpu.VMEM((TAPS * CH, BRK * LANES), BF),
            pltpu.VMEM((8 * CH, BRK * CH), BF),
            pltpu.VMEM((BRK * CH, 2 * VOX), BF),
        ],
        compiler_params=pltpu.CompilerParams(vmem_limit_bytes=24 << 20),
        name="outer",
    )(
        neighbours,
        coarse_map,
        device.reshape(1).astype(jnp.int32),
        base,
        from_below,
        from_above,
        occupancy,
        conv_weight,
        stride_weight,
        bias,
    )
    arrived = lax.ppermute(leave, "grp", [(i, i ^ 1) for i in range(groups)])
    return fine, (stay + arrived)[None]


def solution(mesh):
    both = ("bricks", "grp")
    return jax.shard_map(
        shards,
        mesh=mesh,
        in_specs=(
            P(both, None, None),
            P(both, None),
            P(both, None),
            P(both),
            P(),
            P(),
            P(),
            P(),
            P(),
        ),
        out_specs=(P(both, None, None), P(both, None, None)),
        check_vma=False,
    )
```

time: 224 us -> 27.5 us (0.12)
  local copies, waits for them, and re-layouts: 128 us -> 1.3 us
  other arithmetic: 72.9 us -> 0.67 us
  Pallas kernels: 0 us -> 10.9 us
  matrix products: 6.84 us -> 0 us
    reshape x27 -> x0, local copies, waits for them, and re-layouts: 66.3 us -> none  [the longest x26 55.3 us: convolve(): taps.append(window.reshape(bricks_here, channels, 512))]
    gather x30 -> x0, local copies, waits for them, and re-layouts: 27 us -> none  [the longest x26 24.2 us: fetch(): rows = jnp.take(source, jnp.clip(target - base, 0, local_count - 1), axis=0)]
    mul x26 -> x0, other arithmetic: 20.2 us -> none  [fetch(): return piece * keep[:, None, None, None, None]]
    concatenate x7 -> x0, other arithmetic: 17.7 us -> none  [the longest x2 10.7 us: assemble(): return jnp.concatenate(planes, axis=2)]
    convert_element_type x30 -> x0, other arithmetic: 13.5 us -> none  [the longest x26 9.82 us: fetch(): keep = (target >= 0).astype(piece.dtype)]
    slice x7 -> x0, local copies, waits for them, and re-layouts: 12.3 us -> none  [the longest x4 11.4 us: convolve(): padded[:, :, start_x:start_x + 8, start_y:start_y + 8, start_z:start_z + 8]]
    pallas_call x0 -> x3, Pallas kernels: none -> 10.9 us  [the longest x1 5.4 us: shards(): pl.pallas_call(inner_kernel, in_specs=[smem, vmem, vmem, vmem, vmem, vmem...]
    gather x28 -> x0, other arithmetic: 10.7 us -> none
  transfers between devices with their start and end apart: 4 -> 3, of which waited for: 0 -> 1; matrix products, arithmetic and copies ran while one was open for 79% -> 0% of each run, Pallas kernels for 0% -> 20%
where the time goes in v1:
time: 27.5 us; the launch traced here: 27.3 us
  starting transfers between devices  12.6 us (46%)
  Pallas kernels  10.9 us (40%)
  local copies, waits for them, and re-layouts  1.3 us (5%)
  waiting for transfers between devices  0.99 us (4%)
  between operations  0.77 us (3%)
  other arithmetic  0.67 us (2%)
    ppermute x1, starting transfers between devices, shards(): arrived = lax.ppermute(leave, 'grp', [(i, i ^ 1) for i in range(groups)])  6.84 us
    pallas_call x1, Pallas kernels, shards(): pl.pallas_call(inner_kernel, in_specs=[smem, vmem, vmem, vmem, vmem, vmem...  5.4 us
    ppermute x1, starting transfers between devices, shards(): from_below = lax.ppermute(up, ('bricks', 'grp'), pairs)  3.88 us
    pallas_call x1, Pallas kernels, shards(): pl.pallas_call(outer_kernel, in_specs=[smem, smem, smem] + [vmem] * 7, ou...  3.56 us
    pallas_call x1, Pallas kernels, shards(): pl.pallas_call(faces_kernel, grid=(1,), in_specs=[pl.BlockSpec((BRK, CH,...  1.94 us
    ppermute x1, starting transfers between devices, shards(): lax.ppermute(down, ('bricks', 'grp'), [(j, i) for i, j in pairs])  1.92 us
    unnamed x18, local copies, waits for them, and re-layouts  1.3 us
    ppermute x1, waiting for transfers between devices, shards(): arrived = lax.ppermute(leave, 'grp', [(i, i ^ 1) for i in range(groups)])  0.99 us
  transfers between devices with their start and end apart: 3, of which 1 were waited for; matrix products, arithmetic and copies ran while one was open for 0% of the time, Pallas kernels for 20%

profile of v1, /device:TPU:7, one launch (start us, length us, event | category | flops | bytes accessed | tf_op | source)
XLA Modules:
  0.0 27.3 jit_solution(7752977661766728919)
XLA Ops:
  0.6 0.0 copy-start
  0.6 0.0 copy-start.1
  0.6 0.0 copy-start.8
  0.7 1.9 %faces.1 = (bf16[8,64,128]{2,1,0:T(8,128)(2,1)}, bf16[8,64,128]{2,1,0:T(8,128)(2,1)}) custom-call(bf16[8,64,512]{2,1,0:T(8,128)(2,1)} %high_ref.1, bf16[8,64,512]{2,1,0:T(8,128)(2,1)} %high_ref.1, s32[8,512]{1,0:T(8,128)} %occ_ref.3, s32[8,512]{1,0:T(8,128)} %occ_ref.3, f32[1,64]{1,0:T(1,128)} %bitcast.6), custom_call_target="tpu_custom_call" | custom-call | tf_op jit(solution)/shard_map/faces/pallas_call | solution.py:275
  2.6 3.9 %collective-permute-start = (bf16[8,64,128]{2,1,0:T(8,128)(2,1)}, bf16[8,64,128]{2,1,0:T(8,128)(2,1)S(1)}, u32[]{:S(2)}, u32[]{:S(2)}) collective-permute-start(bf16[8,64,128]{2,1,0:T(8,128)(2,1)} %get-tuple-element.7), channel_id=1, source_target_pairs={{0,1},{1,2},{2,3},{3,4},{4,5},{5,6},{6,7},{7,8},{8,9},{9,10},{10,1... | collective-permute-start | bytes 393224 | tf_op jit(solution)/shard_map/ppermute | solution.py:291
  6.5 1.9 %collective-permute-start.1 = (bf16[8,64,128]{2,1,0:T(8,128)(2,1)}, bf16[8,64,128]{2,1,0:T(8,128)(2,1)S(1)}, u32[]{:S(2)}, u32[]{:S(2)}) collective-permute-start(bf16[8,64,128]{2,1,0:T(8,128)(2,1)} %get-tuple-element.8), channel_id=1, source_target_pairs={{1,0},{2,1},{3,2},{4,3},{5,4},{6,5},{7,6},{8,7},{9,8},{10,9},{11,1... | collective-permute-start | bytes 393224 | tf_op jit(solution)/shard_map/ppermute | solution.py:292
  8.4 0.0 copy-start.4
  8.4 0.0 copy-start.5
  8.5 0.0 copy-done
  8.5 0.0 copy-done.1
  8.5 0.0 copy-done.8
  8.5 0.6 %copy-done.4 = s32[8,26]{1,0:T(8,128)S(1)} copy-done((s32[8,26]{1,0:T(8,128)S(1)}, s32[8,26]{1,0:T(8,128)}, u32[]{:S(2)}) %copy-start.4) | copy-done | bytes 856
  9.1 5.4 %inner.1.base_ref = f32[8,64,512]{2,1,0:T(8,128)S(1)} custom-call(s32[8,26]{1,0:T(8,128)S(1)} %copy-done.4, bf16[8,64,512]{2,1,0:T(8,128)(2,1)S(1)} %copy-done, s32[8,512]{1,0:T(8,128)S(1)} %copy-done.2, f32[1,64]{1,0:T(1,128)S(1)} %bitcast.7, f32[1,64]{1,0:T(1,128)S(1)} %bitcast.9, bf16[27,64,64]{2,1,0:T(8,128)(2,1)S(1)} %copy-done.1), custom_call_target="tpu_custom_call" | custom-call | flops 905969664 | bytes 2097152 | tf_op jit(solution)/shard_map/inner/pallas_call | solution.py:294
  14.5 0.0 collective-permute-done.up_ref
  14.5 0.0 collective-permute-done.1.down_ref
  14.6 0.0 copy-start.6
  14.6 0.0 copy-start.7
  14.6 0.0 copy-done.3
  14.6 0.6 %copy-done.6 = s32[8]{0:T(128)S(1)} copy-done((s32[8]{0:T(128)S(1)}, s32[8]{0:T(128)}, u32[]{:S(2)}) %copy-start.6) | copy-done | bytes 56
  15.2 0.0 copy-done.7
  15.2 3.6 %outer.1 = (bf16[8,64,512]{2,1,0:T(8,128)(2,1)}, bf16[128,512]{1,0:T(8,128)(2,1)S(1)}, bf16[128,512]{1,0:T(8,128)(2,1)S(1)}) custom-call(s32[8,26]{1,0:T(8,128)S(1)} %copy-done.4, s32[8]{0:T(128)S(1)} %copy-done.6, s32[1]{0:T(128)} %bitcast.dev_ref, f32[8,64,512]{2,1,0:T(8,128)S(1)} %inner.1.base_ref, bf16[8,64,128]{2,1,0:T(8,128)(2,1)S(1)} %collective-permute-done.up_ref, ...), custom_call_target="tpu_custom_call" | custom-call | tf_op jit(solution)/shard_map/outer/pallas_call | solution.py:311
  18.8 6.8 %collective-permute-start.2 = (bf16[128,512]{1,0:T(8,128)(2,1)S(1)}, bf16[128,512]{1,0:T(8,128)(2,1)S(1)}, u32[]{:S(2)}, u32[]{:S(2)}) collective-permute-start(bf16[128,512]{1,0:T(8,128)(2,1)S(1)} %get-tuple-element.11), channel_id=1, source_target_pairs={{0,1},{1,0},{2,3},{3,2},{4,5},{5,4},{6,7},{7,6},{8,9},{9,8},{10,11... | collective-permute-start | bytes 393224 | tf_op jit(solution)/shard_map/ppermute | solution.py:342
  25.6 1.0 %collective-permute-done.2 = bf16[128,512]{1,0:T(8,128)(2,1)S(1)} collective-permute-done((bf16[128,512]{1,0:T(8,128)(2,1)S(1)}, bf16[128,512]{1,0:T(8,128)(2,1)S(1)}, u32[]{:S(2)}, u32[]{:S(2)}) %collective-permute-start.2) | collective-permute-done | bytes 131104 | tf_op jit(solution)/shard_map/ppermute | solution.py:342
  26.6 0.7 %add_bitcast_fusion = bf16[1,128,512]{2,1,0:T(8,128)(2,1)} fusion(bf16[128,512]{1,0:T(8,128)(2,1)S(1)} %get-tuple-element.10, bf16[128,512]{1,0:T(8,128)(2,1)S(1)} %collective-permute-done.2), kind=kLoop, calls=%fused_computation | loop fusion | flops 65536 | bytes 393216 | tf_op jit(solution)/shard_map/broadcast_in_dim | solution.py:343
  (4 shorter events, 0.0 us)
Async XLA Ops:
  0.6 7.8 %copy-start = (bf16[8,64,512]{2,1,0:T(8,128)(2,1)S(1)}, bf16[8,64,512]{2,1,0:T(8,128)(2,1)}, u32[]{:S(2)}) copy-start(bf16[8,64,512]{2,1,0:T(8,128)(2,1)} %high_ref.1) | copy-start | bytes 1572868
  0.6 7.8 %copy-start.1 = (bf16[27,64,64]{2,1,0:T(8,128)(2,1)S(1)}, bf16[27,64,64]{2,1,0:T(8,128)(2,1)}, u32[]{:S(2)}) copy-start(bf16[27,64,64]{2,1,0:T(8,128)(2,1)} %weight_ref.3) | copy-start | bytes 663556
  0.6 7.8 %copy-start.8 = (f32[64]{0:T(128)S(1)}, f32[64]{0:T(128)}, u32[]{:S(2)}) copy-start(f32[64]{0:T(128)} %param.14) | copy-start | bytes 772
  2.6 5.9 %copy-start.2 = (s32[8,512]{1,0:T(8,128)S(1)}, s32[8,512]{1,0:T(8,128)}, u32[]{:S(2)}) copy-start(s32[8,512]{1,0:T(8,128)} %occ_ref.3) | copy-start | bytes 49156
  2.6 11.9 %collective-permute-start = (bf16[8,64,128]{2,1,0:T(8,128)(2,1)}, bf16[8,64,128]{2,1,0:T(8,128)(2,1)S(1)}, u32[]{:S(2)}, u32[]{:S(2)}) collective-permute-start(bf16[8,64,128]{2,1,0:T(8,128)(2,1)} %get-tuple-element.7), channel_id=1, source_target_pairs={{0,1},{1,2},{2,3},{3,4},{4,5},{5,6},{6,7},{7,8},{8,9},{9,10},{10,1... | collective-permute-start | bytes 393224 | tf_op jit(solution)/shard_map/ppermute | solution.py:291
  6.5 8.1 %collective-permute-start.1 = (bf16[8,64,128]{2,1,0:T(8,128)(2,1)}, bf16[8,64,128]{2,1,0:T(8,128)(2,1)S(1)}, u32[]{:S(2)}, u32[]{:S(2)}) collective-permute-start(bf16[8,64,128]{2,1,0:T(8,128)(2,1)} %get-tuple-element.8), channel_id=1, source_target_pairs={{1,0},{2,1},{3,2},{4,3},{5,4},{6,5},{7,6},{8,7},{9,8},{10,9},{11,1... | collective-permute-start | bytes 393224 | tf_op jit(solution)/shard_map/ppermute | solution.py:292
  8.4 0.7 %copy-start.4 = (s32[8,26]{1,0:T(8,128)S(1)}, s32[8,26]{1,0:T(8,128)}, u32[]{:S(2)}) copy-start(s32[8,26]{1,0:T(8,128)} %nb_ref.3) | copy-start | bytes 2500
  8.4 0.7 %copy-start.5 = (f32[64]{0:T(128)S(1)}, f32[64]{0:T(128)}, u32[]{:S(2)}) copy-start(f32[64]{0:T(128)} %param.13) | copy-start | bytes 772
  9.1 5.5 %copy-start.3 = (bf16[8,64,128]{2,1,0:T(8,128)(2,1)S(1)}, bf16[8,64,128]{2,1,0:T(8,128)(2,1)}, u32[]{:S(2)}) copy-start(bf16[8,64,128]{2,1,0:T(8,128)(2,1)} %stride_ref.1) | copy-start | bytes 393220
  14.6 0.7 %copy-start.6 = (s32[8]{0:T(128)S(1)}, s32[8]{0:T(128)}, u32[]{:S(2)}) copy-start(s32[8]{0:T(128)} %map_ref.1) | copy-start | bytes 100
  14.6 0.7 %copy-start.7 = (f32[128]{0:T(128)S(1)}, f32[128]{0:T(128)}, u32[]{:S(2)}) copy-start(f32[128]{0:T(128)} %param.17) | copy-start | bytes 1540
  18.8 7.8 %collective-permute-start.2 = (bf16[128,512]{1,0:T(8,128)(2,1)S(1)}, bf16[128,512]{1,0:T(8,128)(2,1)S(1)}, u32[]{:S(2)}, u32[]{:S(2)}) collective-permute-start(bf16[128,512]{1,0:T(8,128)(2,1)S(1)} %get-tuple-element.11), channel_id=1, source_target_pairs={{0,1},{1,0},{2,3},{3,2},{4,5},{5,4},{6,7},{7,6},{8,9},{9,8},{10,11... | collective-permute-start | bytes 393224 | tf_op jit(solution)/shard_map/ppermute | solution.py:342

commit v2 on v1

v2 whole, which is shorter than its diff:
```python
import jax
import jax.numpy as jnp
import ml_dtypes
import numpy as np
from jax import lax
from jax.experimental import pallas as pl
from jax.experimental.pallas import tpu as pltpu
from jax.sharding import PartitionSpec as P

BF = jnp.bfloat16
F32 = jnp.float32
EPS = 1e-06
BRK = 8
CH = 64
CH2 = 128
VOX = 512
LANES = 128
TAPS = 9

LOADED = range(8)

ROLLS = (0, 64, 8, 120, 72, 56)
PLAIN, SWAP, UP, DOWN, SWAP_UP, SWAP_DOWN = range(6)


def column(row):
    n = row.shape[1]
    wide = jnp.broadcast_to(row, (n, n))
    on = lax.broadcasted_iota(jnp.int32, (n, n), 0) == lax.broadcasted_iota(jnp.int32, (n, n), 1)
    return jnp.sum(jnp.where(on, wide, 0.0), axis=1, keepdims=True)


def activate(x, occupied, gain):
    scale = lax.rsqrt(jnp.mean(x * x, axis=0, keepdims=True) + EPS)
    normed = x * scale * gain
    return (normed * jax.nn.sigmoid(normed) * occupied).astype(BF)


def position(dx, dy, dz):
    place = 9 * (dx + 1) + 3 * (dy + 1) + (dz + 1)
    return place - 1 if place > 13 else place


def slot(nb_ref, brick, dx, dy, dz):
    target = nb_ref[brick, position(dx, dy, dz)]
    return jnp.where(target < 0, BRK, target & (BRK - 1))


def lane_masks():
    lane = lax.broadcasted_iota(jnp.int32, (CH, LANES), 1)
    z = lane & 7
    y = (lane >> 3) & 7
    return z == 0, z == 7, y == 0, y == 7, lane < 64


def first_stage(take, masks):
    z0, z7, y0, y7, _ = masks
    centre = take(PLAIN, 0, 0)
    edge = jnp.where(y0, take(SWAP, 1, 0), take(SWAP, -1, 0))
    edge_up = jnp.where(y0, take(SWAP_UP, -1, 1), take(SWAP_UP, 1, 1))
    edge_down = jnp.where(y7, take(SWAP_DOWN, 1, -1), take(SWAP_DOWN, -1, -1))
    middle = (
        pltpu.roll(jnp.where(z7, take(DOWN, 0, -1), centre), 1, 1),
        centre,
        pltpu.roll(jnp.where(z0, take(UP, 0, 1), centre), 127, 1),
    )
    edges = (
        pltpu.roll(jnp.where(z7, edge_down, edge), 1, 1),
        edge,
        pltpu.roll(jnp.where(z0, edge_up, edge), 127, 1),
    )
    return middle, edges


def second_stage(parts, masks, store):
    _, _, y0, y7, _ = masks
    middle, edges = parts
    for c in range(3):
        store(c, pltpu.roll(jnp.where(y7, edges[c], middle[c]), 8, 1))
        store(3 + c, middle[c])
        store(6 + c, pltpu.roll(jnp.where(y0, edges[c], middle[c]), 120, 1))


def halo_stage(raw, masks):
    _, _, y0, _, _ = masks
    edge = pltpu.roll(jnp.where(y0, raw(1, 0), raw(-1, 0)), ROLLS[SWAP], 1)
    edge_up = pltpu.roll(jnp.where(y0, raw(1, 1), raw(-1, 1)), ROLLS[SWAP_UP], 1)
    edge_down = pltpu.roll(jnp.where(y0, raw(1, -1), raw(-1, -1)), ROLLS[SWAP_DOWN], 1)
    up = pltpu.roll(raw(0, 1), ROLLS[UP], 1)
    down = pltpu.roll(raw(0, -1), ROLLS[DOWN], 1)
    return raw(0, 0), edge, edge_up, edge_down, up, down


def halo_second(parts, masks):
    z0, z7, _, _, _ = masks
    centre, edge, edge_up, edge_down, up, down = parts
    middle = (
        pltpu.roll(jnp.where(z7, down, centre), 1, 1),
        centre,
        pltpu.roll(jnp.where(z0, up, centre), 127, 1),
    )
    edges = (
        pltpu.roll(jnp.where(z7, edge_down, edge), 1, 1),
        edge,
        pltpu.roll(jnp.where(z0, edge_up, edge), 127, 1),
    )
    return middle, edges


def columns(j):
    return slice(j * LANES, (j + 1) * LANES)


def faces_kernel(*refs):
    count = len(LOADED)
    sources, face_ref, kept, sems = refs[:count], refs[count], refs[count + 1 : -1], refs[-1]
    copies = [
        pltpu.make_async_copy(source, target, sems.at[k])
        for k, (source, target) in enumerate(zip(sources, kept))
    ]
    for copy in copies:
        copy.start()
    for copy in copies[:3]:
        copy.wait()
    features_ref, occ_ref, gain_ref = kept[:3]
    gain = column(gain_ref[...])
    low = lax.broadcasted_iota(jnp.int32, (CH, LANES), 1) < 64
    for i in range(BRK):
        first, last = features_ref[i, :, columns(0)], features_ref[i, :, columns(3)]
        x = jnp.where(low, first.astype(F32), last.astype(F32))
        row = slice(i, i + 1)
        occupied = jnp.where(low[:1], occ_ref[row, columns(0)], occ_ref[row, columns(3)])
        face_ref[i] = activate(x, occupied.astype(F32), gain)
    for copy in copies[3:]:
        copy.wait()


def inner_kernel(
    nb_ref, features_ref, occ_ref, gain_ref, shift_ref, weight_ref, base_ref,
    acts, wide, stack, ybuf, nb, sem,
):
    copy = pltpu.make_async_copy(nb_ref, nb, sem)
    copy.start()
    gain = column(gain_ref[...])
    shift = column(shift_ref[...])
    masks = lane_masks()
    low = lax.broadcasted_iota(jnp.int32, (CH, LANES), 1) < 64
    for kind in range(len(ROLLS)):
        acts[kind, BRK] = jnp.zeros((CH, VOX), BF)

    def rotate(i):
        for j in range(4):
            piece = acts[PLAIN, i, :, columns(j)]
            for kind in range(1, len(ROLLS)):
                acts[kind, i, :, columns(j)] = pltpu.roll(piece, ROLLS[kind], 1)

    for i in range(BRK):
        occupied = occ_ref[i : i + 1, :].astype(F32)
        acts[PLAIN, i] = activate(features_ref[i].astype(F32), occupied, gain)
        if i > 0:
            rotate(i - 1)
    for a in range(3):
        wide[a * CH : (a + 1) * CH, :] = (
            weight_ref[TAPS * a : TAPS * (a + 1)].reshape(TAPS * CH, CH).T
        )
    rotate(BRK - 1)
    copy.wait()

    def product(i, half):
        lanes = slice(2 * half * LANES, 2 * (half + 1) * LANES)
        ybuf[i % 2, :, lanes] = jnp.dot(
            wide[...], stack[i % 2, :, lanes], preferred_element_type=F32
        )

    def finish(i, half):
        y = ybuf.at[i % 2]
        for j in (2 * half, 2 * half + 1):
            to_high = y[2 * CH :, columns(j)]
            if j > 0:
                to_high = to_high + y[:CH, columns(j - 1)]
            to_low = y[:CH, columns(j)]
            if j < 3:
                to_low = to_low + y[2 * CH :, columns(j + 1)]
            moved = pltpu.roll(jnp.where(low, to_low, to_high), 64, 1)
            total = y[CH : 2 * CH, columns(j)] + features_ref[i, :, columns(j)].astype(F32)
            base_ref[i, :, columns(j)] = (total + shift) + moved

    waiting = None
    for i in range(BRK + 1):
        if i < BRK:
            slots = {
                (dy, dz): i if (dy, dz) == (0, 0) else slot(nb, i, 0, dy, dz)
                for dy in (-1, 0, 1)
                for dz in (-1, 0, 1)
            }
        for j in range(4):
            parts = None
            if i < BRK:
                parts = first_stage(
                    lambda kind, dy, dz: acts[kind, slots[dy, dz], :, columns(j)], masks
                )
            if waiting is not None:
                oi, oj, old = waiting

                def store(tap, piece):
                    stack[oi % 2, tap * CH : (tap + 1) * CH, columns(oj)] = piece

                second_stage(old, masks, store)
                if oj == 1:
                    product(oi, 0)
                if oj == 3:
                    product(oi, 1)
            waiting = (i, j, parts) if parts is not None else None
            if i > 0 and j == 1:
                finish(i - 1, 0)
            if i > 0 and j == 2:
                finish(i - 1, 1)


def outer_kernel(
    nb_ref, map_ref, base_ref, chip_ref, far_ref, occ_ref, weight_ref, stride_ref, bias_ref,
    sort_ref, entry_ref, place_ref,
    fine_ref, stay_ref, leave_ref,
    halo, wide, wide2, stack, picked, placing, mask, nb, map_, order, sems,
):
    copies = [
        pltpu.make_async_copy(nb_ref, nb, sems.at[0]),
        pltpu.make_async_copy(map_ref, map_, sems.at[1]),
    ]
    for copy in copies:
        copy.start()
    groups = lax.axis_size("grp")
    device = lax.axis_index("bricks") * groups + lax.axis_index("grp")
    odd = lax.rem(device, 2)
    masks = lane_masks()
    low = masks[4]
    low32 = lax.broadcasted_iota(jnp.int32, (CH, LANES), 1) < 64
    for i in range(BRK):
        halo[odd, i] = chip_ref[i]
        halo[1 - odd, i] = far_ref[i]
    for i in range(BRK):
        mask[i] = occ_ref[i : i + 1, :].astype(F32)
    halo[0, BRK] = jnp.zeros((CH, LANES), BF)
    halo[1, BRK] = jnp.zeros((CH, LANES), BF)
    for row, a in enumerate((0, 2)):
        wide[row * CH : (row + 1) * CH, :] = (
            weight_ref[TAPS * a : TAPS * (a + 1)].reshape(TAPS * CH, CH).T
        )
    wide2[...] = stride_ref[...].reshape(8 * CH, CH2).T
    for copy in copies:
        copy.wait()
    staying, leaving = jnp.int32(0), jnp.int32(BRK // 2)
    for i in range(BRK):
        stays = (map_[0, i] >> 3) == device
        order[jnp.where(stays, staying, leaving)] = i
        staying = staying + stays.astype(jnp.int32)
        leaving = leaving + 1 - stays.astype(jnp.int32)
    brick = [order[k] for k in range(BRK)]

    def raw_of(i):
        def raw(dy, dz):
            return jnp.where(
                low,
                halo[0, slot(nb, i, 1, dy, dz)],
                halo[1, slot(nb, i, -1, dy, dz)],
            )

        return raw

    def finish(pair):
        lanes = slice(2 * pair * LANES, 2 * (pair + 1) * LANES)
        edge = jnp.dot(wide[...], stack[:, lanes], preferred_element_type=F32)
        for k in range(2):
            i = brick[2 * pair + k]
            mine = edge[:, columns(k)]
            moved = pltpu.roll(jnp.where(low32, mine[CH:], mine[:CH]), 64, 1)
            for j in range(4):
                total = base_ref[i, :, columns(j)]
                if j == 0:
                    total = total + jnp.where(low32, moved, 0.0)
                if j == 3:
                    total = total + jnp.where(low32, 0.0, moved)
                occupied = mask[i, :, columns(j)]
                fine_ref[i, :, columns(j)] = (occupied * total).astype(BF)

    def sort(pair):
        both = jnp.concatenate([fine_ref[brick[2 * pair]], fine_ref[brick[2 * pair + 1]]], axis=0)
        by_tap = jnp.dot(both, sort_ref[...], preferred_element_type=F32).astype(BF)
        for j in range(4):
            one, two = by_tap[:CH, columns(j)], by_tap[CH:, columns(j)]
            picked[2 * j * CH : (2 * j + 1) * CH, columns(pair)] = jnp.where(
                low, one, pltpu.roll(two, 64, 1)
            )
            picked[(2 * j + 1) * CH : (2 * j + 2) * CH, columns(pair)] = jnp.where(
                low, pltpu.roll(one, 64, 1), two
            )

    first, second = None, None
    for k in range(BRK + 2):
        now = halo_stage(raw_of(brick[k]), masks) if k < BRK else None
        later = halo_second(first, masks) if first is not None else None
        if second is not None:
            spot = k - 2

            def store(tap, piece):
                stack[tap * CH : (tap + 1) * CH, columns(spot)] = piece

            second_stage(second, masks, store)
            if spot % 2 == 1:
                finish(spot // 2)
                if spot >= 3:
                    sort(spot // 2 - 1)
        first, second = now, later
    sort(BRK // 2 - 1)
    for k in range(BRK):
        which = map_[0, brick[k]] & 7
        row = place_ref[which].astype(BF)
        placing[k * CH : (k + 1) * CH, :] = entry_ref[...] * row
    octant = jnp.dot(wide2[...], picked[...], preferred_element_type=F32)
    octant = (octant + column(bias_ref[...])).astype(BF)
    half = BRK // 2 * CH
    leave_ref[...] = jnp.dot(
        octant[:, half:], placing[half:, :], preferred_element_type=F32
    ).astype(BF)
    stay_ref[...] = jnp.dot(
        octant[:, :half], placing[:half, :], preferred_element_type=F32
    ).astype(BF)


def tables():
    voxel = np.arange(VOX)
    x, y, z = voxel >> 6, (voxel >> 3) & 7, voxel & 7
    lane = 64 * (4 * (x & 1) + 2 * (y & 1) + (z & 1)) + 16 * (x >> 1) + 4 * (y >> 1) + (z >> 1)
    sort = (lane[:, None] == voxel[None, :]).astype(ml_dtypes.bfloat16)
    source = 16 * (x & 3) + 4 * (y & 3) + (z & 3)
    entry = (np.arange(64)[:, None] == source[None, :]).astype(ml_dtypes.bfloat16)
    octant = 4 * (x >> 2) + 2 * (y >> 2) + (z >> 2)
    place = (np.arange(8)[:, None, None] == octant).astype(np.float32)
    return sort, entry, place


def shards(
    features,
    occupancy,
    neighbours,
    coarse_map,
    norm_gain,
    time_shift,
    conv_weight,
    stride_weight,
    coarse_bias,
):
    groups = lax.axis_size("grp")
    total = lax.axis_size("bricks") * groups
    vmem = pl.BlockSpec(memory_space=pltpu.VMEM)

    loaded = (
        features,
        occupancy,
        norm_gain.reshape(1, CH),
        time_shift.reshape(1, CH),
        conv_weight,
        neighbours,
        coarse_map.reshape(1, BRK),
        coarse_bias.reshape(1, CH2),
    )
    face, features, occupancy, gain, shift, conv_weight, neighbours, coarse_map, bias = (
        pl.pallas_call(
            faces_kernel,
            in_specs=[pl.BlockSpec(memory_space=pltpu.HBM)] * len(loaded),
            out_specs=[vmem] * (1 + len(loaded)),
            out_shape=[jax.ShapeDtypeStruct((BRK, CH, LANES), BF)]
            + [jax.ShapeDtypeStruct(x.shape, x.dtype) for x in loaded],
            scratch_shapes=[pltpu.SemaphoreType.DMA((len(loaded),))],
            compiler_params=pltpu.CompilerParams(vmem_limit_bytes=8 << 20),
            name="faces",
        )(*(pltpu.with_memory_space_constraint(x, pltpu.HBM) for x in loaded))
    )

    chip = lax.ppermute(face, "grp", [(i, i ^ 1) for i in range(groups)])
    across = [(i, i + 1) for i in range(1, total - 1, 2)]
    far = lax.ppermute(face, ("bricks", "grp"), across + [(j, i) for i, j in across])

    base = pl.pallas_call(
        inner_kernel,
        in_specs=[vmem] * 6,
        out_specs=vmem,
        out_shape=jax.ShapeDtypeStruct((BRK, CH, VOX), F32),
        scratch_shapes=[
            pltpu.VMEM((len(ROLLS), BRK + 1, CH, VOX), BF),
            pltpu.VMEM((3 * CH, TAPS * CH), BF),
            pltpu.VMEM((2, TAPS * CH, VOX), BF),
            pltpu.VMEM((2, 3 * CH, VOX), F32),
            pltpu.SMEM((BRK, 26), jnp.int32),
            pltpu.SemaphoreType.DMA,
        ],
        compiler_params=pltpu.CompilerParams(vmem_limit_bytes=16 << 20),
        cost_estimate=pl.CostEstimate(
            flops=2 * 27 * CH * CH * VOX * BRK, bytes_accessed=2 << 20, transcendentals=0
        ),
        name="inner",
    )(neighbours, features, occupancy, gain, shift, conv_weight)

    sort, entry, place = (jnp.asarray(table) for table in tables())
    fine, stay, leave = pl.pallas_call(
        outer_kernel,
        in_specs=[vmem] * 12,
        out_specs=[vmem] * 3,
        out_shape=(
            jax.ShapeDtypeStruct((BRK, CH, VOX), BF),
            jax.ShapeDtypeStruct((CH2, VOX), BF),
            jax.ShapeDtypeStruct((CH2, VOX), BF),
        ),
        scratch_shapes=[
            pltpu.VMEM((2, BRK + 1, CH, LANES), BF),
            pltpu.VMEM((2 * CH, TAPS * CH), BF),
            pltpu.VMEM((CH2, 8 * CH), BF),
            pltpu.VMEM((TAPS * CH, BRK * LANES), BF),
            pltpu.VMEM((8 * CH, BRK * CH), BF),
            pltpu.VMEM((BRK * CH, VOX), BF),
            pltpu.VMEM((BRK, 1, VOX), F32),
            pltpu.SMEM((BRK, 26), jnp.int32),
            pltpu.SMEM((1, BRK), jnp.int32),
            pltpu.SMEM((BRK,), jnp.int32),
            pltpu.SemaphoreType.DMA((2,)),
        ],
        compiler_params=pltpu.CompilerParams(vmem_limit_bytes=16 << 20),
        name="outer",
    )(
        neighbours,
        coarse_map,
        base,
        chip,
        far,
        occupancy,
        conv_weight,
        stride_weight,
        bias,
        sort,
        entry,
        place,
    )
    arrived = lax.ppermute(leave, "grp", [(i, i ^ 1) for i in range(groups)])
    return fine, (stay + arrived)[None]


def solution(mesh):
    both = ("bricks", "grp")
    return jax.shard_map(
        shards,
        mesh=mesh,
        in_specs=(
            P(both, None, None),
            P(both, None),
            P(both, None),
            P(both),
            P(),
            P(),
            P(),
            P(),
            P(),
        ),
        out_specs=(P(both, None, None), P(both, None, None)),
        check_vma=False,
    )
```

time: 27.5 us -> 22.2 us (0.81)
  Pallas kernels: 10.9 us -> 8.56 us
  starting transfers between devices: 12.6 us -> 10.8 us
  local copies, waits for them, and re-layouts: 1.3 us -> 0.01 us
  waiting for transfers between devices: 0.99 us -> 1.31 us
    ppermute x1, starting transfers between devices: 6.84 us -> 0.13 us  [shards(): arrived = lax.ppermute(leave, 'grp', [(i, i ^ 1) for i in range(groups)])]
    ppermute x2, starting transfers between devices: 5.8 us -> 10.7 us  [the longest x1 6.92 us: shards(): chip = lax.ppermute(face, 'grp', [(i, i ^ 1) for i in range(groups)])]
    pallas_call x3, Pallas kernels: 10.9 us -> 8.56 us  [the longest x1 3.63 us: shards(): pl.pallas_call(inner_kernel, in_specs=[vmem] * 6, out_specs=vmem, out_sha...]
    unnamed x18 -> x8, local copies, waits for them, and re-layouts: 1.3 us -> 0.01 us
    ppermute x1, waiting for transfers between devices: 0.99 us -> 1.3 us  [shards(): arrived = lax.ppermute(leave, 'grp', [(i, i ^ 1) for i in range(groups)])]
  transfers between devices with their start and end apart: 3 -> 3, of which waited for: 1 -> 1; matrix products, arithmetic and copies ran while one was open for 0% -> 0% of each run, Pallas kernels for 20% -> 16%
where the time goes in v2:
time: 22.2 us; the launch traced here: 22.1 us
  starting transfers between devices  10.8 us (49%)
  Pallas kernels  8.56 us (39%)
  waiting for transfers between devices  1.31 us (6%)
  between operations  0.72 us (3%)
  other arithmetic  0.67 us (3%)
    ppermute x1, starting transfers between devices, shards(): chip = lax.ppermute(face, 'grp', [(i, i ^ 1) for i in range(groups)])  6.92 us
    ppermute x1, starting transfers between devices, shards(): lax.ppermute(face, ('bricks', 'grp'), across + [(j, i) for i, j in across])  3.77 us
    pallas_call x1, Pallas kernels, shards(): pl.pallas_call(inner_kernel, in_specs=[vmem] * 6, out_specs=vmem, out_sha...  3.63 us
    pallas_call x1, Pallas kernels, shards(): pl.pallas_call(outer_kernel, in_specs=[vmem] * 12, out_specs=[vmem] * 3,...  3.63 us
    ppermute x1, waiting for transfers between devices, shards(): arrived = lax.ppermute(leave, 'grp', [(i, i ^ 1) for i in range(groups)])  1.3 us
    pallas_call x1, Pallas kernels, shards(): pl.pallas_call(faces_kernel, in_specs=[pl.BlockSpec(memory_space=pltpu.HB...  1.3 us
    broadcast_in_dim x1, other arithmetic, shards(): return (fine, (stay + arrived)[None])  0.67 us
  transfers between devices with their start and end apart: 3, of which 1 were waited for; matrix products, arithmetic and copies ran while one was open for 0% of the time, Pallas kernels for 16%

profile of v2, /device:TPU:7, one launch (start us, length us, event | category | flops | bytes accessed | tf_op | source)
XLA Modules:
  0.0 22.1 jit_solution(6585944076386767334)
XLA Ops:
  0.6 1.3 %faces.1 = (bf16[8,64,128]{2,1,0:T(8,128)(2,1)S(1)}, bf16[8,64,512]{2,1,0:T(8,128)(2,1)S(1)}, s32[8,512]{1,0:T(8,128)S(1)}, f32[1,64]{1,0:T(1,128)S(1)}, f32[1,6...) custom-call(bf16[8,64,512]{2,1,0:T(8,128)(2,1)} %refs_0_.1, ...), custom_call_target="tpu_custom_call" | custom-call | tf_op jit(solution)/shard_map/faces/pallas_call | solution.py:368
  1.9 3.8 %collective-permute-start.1 = (bf16[8,64,128]{2,1,0:T(8,128)(2,1)S(1)}, bf16[8,64,128]{2,1,0:T(8,128)(2,1)S(1)}, u32[]{:S(2)}, u32[]{:S(2)}) collective-permute-start(bf16[8,64,128]{2,1,0:T(8,128)(2,1)S(1)} %get-tuple-element.21), channel_id=1, source_target_pairs={{1,2},{3,4},{5,6},{7,8},{9,10},{11,12},{13,14},{15,16},{17,18},{19... | collective-permute-start | bytes 393224 | tf_op jit(solution)/shard_map/ppermute | solution.py:382
  5.7 6.9 %collective-permute-start = (bf16[8,64,128]{2,1,0:T(8,128)(2,1)S(1)}, bf16[8,64,128]{2,1,0:T(8,128)(2,1)S(1)}, u32[]{:S(2)}, u32[]{:S(2)}) collective-permute-start(bf16[8,64,128]{2,1,0:T(8,128)(2,1)S(1)} %get-tuple-element.21), channel_id=1, source_target_pairs={{0,1},{1,0},{2,3},{3,2},{4,5},{5,4},{6,7},{7,6},{8,9},{9,8},{10,11... | collective-permute-start | bytes 393224 | tf_op jit(solution)/shard_map/ppermute | solution.py:380
  12.6 0.0 copy-start
  12.6 0.0 copy-start.1
  12.6 0.0 copy-start.2
  12.6 0.0 copy-start.3
  12.6 3.6 %inner.1.base_ref = f32[8,64,512]{2,1,0:T(8,128)S(1)} custom-call(s32[8,26]{1,0:T(8,128)S(1)} %get-tuple-element.14.nb_ref, bf16[8,64,512]{2,1,0:T(8,128)(2,1)S(1)} %get-tuple-element.16.features_ref, s32[8,512]{1,0:T(8,128)S(1)} %get-tuple-element.17.occ_ref, f32[1,64]{1,0:T(1,128)S(1)} %get-tuple-element.18.gain_ref, ...), custom_call_target="tpu_custom_call" | custom-call | flops 905969664 | bytes 2097152 | tf_op jit(solution)/shard_map/inner/pallas_call | solution.py:384
  16.3 0.0 collective-permute-done.1.far_ref
  16.3 0.0 collective-permute-done.chip_ref
  16.3 0.0 copy-done
  16.3 0.0 copy-done.1
  16.3 0.0 copy-done.2
  16.3 0.0 copy-done.3
  16.3 3.6 %outer.1 = (bf16[8,64,512]{2,1,0:T(8,128)(2,1)}, bf16[128,512]{1,0:T(8,128)(2,1)S(1)}, bf16[128,512]{1,0:T(8,128)(2,1)S(1)}) custom-call(s32[8,26]{1,0:T(8,128)S(1)} %get-tuple-element.14.nb_ref, s32[1,8]{1,0:T(1,128)S(1)} %get-tuple-element.15.map_ref, f32[8,64,512]{2,1,0:T(8,128)S(1)} %inner.1.base_ref, ...), custom_call_target="tpu_custom_call" | custom-call | tf_op jit(solution)/shard_map/outer/pallas_call | solution.py:405
  20.0 0.1 collective-permute-start.2
  20.1 1.3 %collective-permute-done.2 = bf16[128,512]{1,0:T(8,128)(2,1)S(1)} collective-permute-done((bf16[128,512]{1,0:T(8,128)(2,1)S(1)}, bf16[128,512]{1,0:T(8,128)(2,1)S(1)}, u32[]{:S(2)}, u32[]{:S(2)}) %collective-permute-start.2) | collective-permute-done | bytes 131104 | tf_op jit(solution)/shard_map/ppermute | solution.py:443
  21.4 0.7 %add_bitcast_fusion = bf16[1,128,512]{2,1,0:T(8,128)(2,1)} fusion(bf16[128,512]{1,0:T(8,128)(2,1)S(1)} %get-tuple-element.24, bf16[128,512]{1,0:T(8,128)(2,1)S(1)} %collective-permute-done.2), kind=kLoop, calls=%fused_computation | loop fusion | flops 65536 | bytes 393216 | tf_op jit(solution)/shard_map/broadcast_in_dim | solution.py:444
Async XLA Ops:
  1.9 14.3 %collective-permute-start.1 = (bf16[8,64,128]{2,1,0:T(8,128)(2,1)S(1)}, bf16[8,64,128]{2,1,0:T(8,128)(2,1)S(1)}, u32[]{:S(2)}, u32[]{:S(2)}) collective-permute-start(bf16[8,64,128]{2,1,0:T(8,128)(2,1)S(1)} %get-tuple-element.21), channel_id=1, source_target_pairs={{1,2},{3,4},{5,6},{7,8},{9,10},{11,12},{13,14},{15,16},{17,18},{19... | collective-permute-start | bytes 393224 | tf_op jit(solution)/shard_map/ppermute | solution.py:382
  5.7 10.6 %collective-permute-start = (bf16[8,64,128]{2,1,0:T(8,128)(2,1)S(1)}, bf16[8,64,128]{2,1,0:T(8,128)(2,1)S(1)}, u32[]{:S(2)}, u32[]{:S(2)}) collective-permute-start(bf16[8,64,128]{2,1,0:T(8,128)(2,1)S(1)} %get-tuple-element.21), channel_id=1, source_target_pairs={{0,1},{1,0},{2,3},{3,2},{4,5},{5,4},{6,7},{7,6},{8,9},{9,8},{10,11... | collective-permute-start | bytes 393224 | tf_op jit(solution)/shard_map/ppermute | solution.py:380
  12.6 3.7 %copy-start = (bf16[512,512]{1,0:T(8,128)(2,1)S(1)}, bf16[512,512]{1,0:T(8,128)(2,1)}, u32[]{:S(2)}) copy-start(bf16[512,512]{1,0:T(8,128)(2,1)} %constant.6.clone.sort_ref) | copy-start | bytes 1572868
  12.6 3.7 %copy-start.1 = (bf16[8,64,128]{2,1,0:T(8,128)(2,1)S(1)}, bf16[8,64,128]{2,1,0:T(8,128)(2,1)}, u32[]{:S(2)}) copy-start(bf16[8,64,128]{2,1,0:T(8,128)(2,1)} %stride_ref.1) | copy-start | bytes 393220
  12.6 3.7 %copy-start.2 = (bf16[64,512]{1,0:T(8,128)(2,1)S(1)}, bf16[64,512]{1,0:T(8,128)(2,1)}, u32[]{:S(2)}) copy-start(bf16[64,512]{1,0:T(8,128)(2,1)} %constant.7.clone.entry_ref) | copy-start | bytes 196612
  12.6 3.7 %copy-start.3 = (f32[8,1,512]{2,1,0:T(1,128)S(1)}, f32[8,1,512]{2,1,0:T(1,128)}, u32[]{:S(2)}) copy-start(f32[8,1,512]{2,1,0:T(1,128)} %constant.8.clone.place_ref) | copy-start | bytes 49156
  20.0 1.4 %collective-permute-start.2 = (bf16[128,512]{1,0:T(8,128)(2,1)S(1)}, bf16[128,512]{1,0:T(8,128)(2,1)S(1)}, u32[]{:S(2)}, u32[]{:S(2)}) collective-permute-start(bf16[128,512]{1,0:T(8,128)(2,1)S(1)} %get-tuple-element.25), channel_id=1, source_target_pairs={{0,1},{1,0},{2,3},{3,2},{4,5},{5,4},{6,7},{7,6},{8,9},{9,8},{10,11... | collective-permute-start | bytes 393224 | tf_op jit(solution)/shard_map/ppermute | solution.py:443

commit v3 on v2

--- a/solution.py
+++ b/solution.py
@@ -206,22 +206,22 @@
                     stack[oi % 2, tap * CH : (tap + 1) * CH, columns(oj)] = piece
 
                 second_stage(old, masks, store)
-                if oj == 1:
-                    product(oi, 0)
-                if oj == 3:
-                    product(oi, 1)
             waiting = (i, j, parts) if parts is not None else None
+            if i < BRK and j == 3:
+                product(i, 0)
             if i > 0 and j == 1:
+                product(i - 1, 1)
+            if i > 0 and j == 2:
                 finish(i - 1, 0)
-            if i > 0 and j == 2:
+            if i > 0 and j == 3:
                 finish(i - 1, 1)
 
 
 def outer_kernel(
     nb_ref, map_ref, base_ref, chip_ref, far_ref, occ_ref, weight_ref, stride_ref, bias_ref,
     sort_ref, entry_ref, place_ref,
-    fine_ref, stay_ref, leave_ref,
-    halo, wide, wide2, stack, picked, placing, mask, nb, map_, order, sems,
+    fine_hbm, stay_ref, leave_ref,
+    fine_ref, halo, wide, wide2, stack, picked, placing, mask, nb, map_, order, sems,
 ):
     copies = [
         pltpu.make_async_copy(nb_ref, nb, sems.at[0]),
@@ -246,7 +246,9 @@
         wide[row * CH : (row + 1) * CH, :] = (
             weight_ref[TAPS * a : TAPS * (a + 1)].reshape(TAPS * CH, CH).T
         )
-    wide2[...] = stride_ref[...].reshape(8 * CH, CH2).T
+    for c in range(2):
+        taps = jnp.concatenate([stride_ref[2 * k + c] for k in range(4)], axis=0)
+        wide2[c] = taps.T
     for copy in copies:
         copy.wait()
     staying, leaving = jnp.int32(0), jnp.int32(BRK // 2)
@@ -283,18 +285,27 @@
                 occupied = mask[i, :, columns(j)]
                 fine_ref[i, :, columns(j)] = (occupied * total).astype(BF)
 
-    def sort(pair):
-        both = jnp.concatenate([fine_ref[brick[2 * pair]], fine_ref[brick[2 * pair + 1]]], axis=0)
-        by_tap = jnp.dot(both, sort_ref[...], preferred_element_type=F32).astype(BF)
-        for j in range(4):
-            one, two = by_tap[:CH, columns(j)], by_tap[CH:, columns(j)]
-            picked[2 * j * CH : (2 * j + 1) * CH, columns(pair)] = jnp.where(
-                low, one, pltpu.roll(two, 64, 1)
+    def sort(half):
+        sorted_ = []
+        for k in range(2):
+            rows = [fine_ref[brick[4 * half + 2 * pair + k]] for pair in range(2)]
+            sorted_.append(
+                jnp.dot(
+                    jnp.concatenate(rows, axis=0), sort_ref[k], preferred_element_type=F32
+                ).astype(BF)
             )
-            picked[(2 * j + 1) * CH : (2 * j + 2) * CH, columns(pair)] = jnp.where(
-                low, pltpu.roll(one, 64, 1), two
-            )
-
+        for pair in range(2):
+            rows = slice(pair * CH, (pair + 1) * CH)
+            for j in range(4):
+                one, two = sorted_[0][rows, columns(j)], sorted_[1][rows, columns(j)]
+                taps = slice(j * CH, (j + 1) * CH)
+                picked[0, taps, columns(2 * half + pair)] = jnp.where(low, one, two)
+                picked[1, taps, columns(2 * half + pair)] = jnp.where(low, two, one)
+
+    for k in range(BRK):
+        which = map_[0, brick[k]] & 7
+        row = place_ref[which].astype(BF)
+        placing[k * CH : (k + 1) * CH, :] = entry_ref[...] * row
     first, second = None, None
     for k in range(BRK + 2):
         now = halo_stage(raw_of(brick[k]), masks) if k < BRK else None
@@ -308,16 +319,20 @@
             second_stage(second, masks, store)
             if spot % 2 == 1:
                 finish(spot // 2)
-                if spot >= 3:
-                    sort(spot // 2 - 1)
+                if spot == 5:
+                    sort(0)
         first, second = now, later
-    sort(BRK // 2 - 1)
-    for k in range(BRK):
-        which = map_[0, brick[k]] & 7
-        row = place_ref[which].astype(BF)
-        placing[k * CH : (k + 1) * CH, :] = entry_ref[...] * row
-    octant = jnp.dot(wide2[...], picked[...], preferred_element_type=F32)
-    octant = (octant + column(bias_ref[...])).astype(BF)
+    out = pltpu.make_async_copy(fine_ref, fine_hbm, sems.at[2])
+    out.start()
+    sort(1)
+    octant = []
+    for pair in range(BRK // 2):
+        even, odd = (
+            jnp.dot(wide2[c], picked[c, :, columns(pair)], preferred_element_type=F32)
+            for c in range(2)
+        )
+        octant.append(even + pltpu.roll(odd, 64, 1))
+    octant = (jnp.concatenate(octant, axis=1) + column(bias_ref[...])).astype(BF)
     half = BRK // 2 * CH
     leave_ref[...] = jnp.dot(
         octant[:, half:], placing[half:, :], preferred_element_type=F32
@@ -325,13 +340,14 @@
     stay_ref[...] = jnp.dot(
         octant[:, :half], placing[:half, :], preferred_element_type=F32
     ).astype(BF)
+    out.wait()
 
 
 def tables():
     voxel = np.arange(VOX)
     x, y, z = voxel >> 6, (voxel >> 3) & 7, voxel & 7
     lane = 64 * (4 * (x & 1) + 2 * (y & 1) + (z & 1)) + 16 * (x >> 1) + 4 * (y >> 1) + (z >> 1)
-    sort = (lane[:, None] == voxel[None, :]).astype(ml_dtypes.bfloat16)
+    sort = np.stack([lane[:, None] == voxel, (lane ^ 64)[:, None] == voxel]).astype(ml_dtypes.bfloat16)
     source = 16 * (x & 3) + 4 * (y & 3) + (z & 3)
     entry = (np.arange(64)[:, None] == source[None, :]).astype(ml_dtypes.bfloat16)
     octant = 4 * (x >> 2) + 2 * (y >> 2) + (z >> 2)
@@ -405,24 +421,25 @@
     fine, stay, leave = pl.pallas_call(
         outer_kernel,
         in_specs=[vmem] * 12,
-        out_specs=[vmem] * 3,
+        out_specs=[pl.BlockSpec(memory_space=pltpu.HBM), vmem, vmem],
         out_shape=(
             jax.ShapeDtypeStruct((BRK, CH, VOX), BF),
             jax.ShapeDtypeStruct((CH2, VOX), BF),
             jax.ShapeDtypeStruct((CH2, VOX), BF),
         ),
         scratch_shapes=[
+            pltpu.VMEM((BRK, CH, VOX), BF),
             pltpu.VMEM((2, BRK + 1, CH, LANES), BF),
             pltpu.VMEM((2 * CH, TAPS * CH), BF),
-            pltpu.VMEM((CH2, 8 * CH), BF),
+            pltpu.VMEM((2, CH2, 4 * CH), BF),
             pltpu.VMEM((TAPS * CH, BRK * LANES), BF),
-            pltpu.VMEM((8 * CH, BRK * CH), BF),
+            pltpu.VMEM((2, 4 * CH, BRK * CH), BF),
             pltpu.VMEM((BRK * CH, VOX), BF),
             pltpu.VMEM((BRK, 1, VOX), F32),
             pltpu.SMEM((BRK, 26), jnp.int32),
             pltpu.SMEM((1, BRK), jnp.int32),
             pltpu.SMEM((BRK,), jnp.int32),
-            pltpu.SemaphoreType.DMA((2,)),
+            pltpu.SemaphoreType.DMA((3,)),
         ],
         compiler_params=pltpu.CompilerParams(vmem_limit_bytes=16 << 20),
         name="outer",

time: 22.2 us -> 21.6 us (0.973)
  Pallas kernels: 8.56 us -> 8 us
    pallas_call x1, Pallas kernels: 3.63 us -> 3.1 us  [shards(): pl.pallas_call(outer_kernel, in_specs=[vmem] * 12, out_specs=[pl.BlockSpe...]
  transfers between devices with their start and end apart: 3 -> 3, of which waited for: 1 -> 1; matrix products, arithmetic and copies ran while one was open for 0% -> 0% of each run, Pallas kernels for 16% -> 17%
where the time goes in v3:
time: 21.6 us; the launch traced here: 21.5 us
  starting transfers between devices  10.8 us (50%)
  Pallas kernels  8 us (37%)
  waiting for transfers between devices  1.3 us (6%)
  between operations  0.72 us (3%)
  other arithmetic  0.67 us (3%)
    ppermute x1, starting transfers between devices, shards(): chip = lax.ppermute(face, 'grp', [(i, i ^ 1) for i in range(groups)])  6.92 us
    ppermute x1, starting transfers between devices, shards(): lax.ppermute(face, ('bricks', 'grp'), across + [(j, i) for i, j in across])  3.77 us
    pallas_call x1, Pallas kernels, shards(): pl.pallas_call(inner_kernel, in_specs=[vmem] * 6, out_specs=vmem, out_sha...  3.6 us
    pallas_call x1, Pallas kernels, shards(): pl.pallas_call(outer_kernel, in_specs=[vmem] * 12, out_specs=[pl.BlockSpe...  3.1 us
    pallas_call x1, Pallas kernels, shards(): pl.pallas_call(faces_kernel, in_specs=[pl.BlockSpec(memory_space=pltpu.HB...  1.3 us
    ppermute x1, waiting for transfers between devices, shards(): arrived = lax.ppermute(leave, 'grp', [(i, i ^ 1) for i in range(groups)])  1.3 us
    broadcast_in_dim x1, other arithmetic, shards(): return (fine, (stay + arrived)[None])  0.67 us
  transfers between devices with their start and end apart: 3, of which 1 were waited for; matrix products, arithmetic and copies ran while one was open for 0% of the time, Pallas kernels for 17%

profile of v3, /device:TPU:7, one launch (start us, length us, event | category | flops | bytes accessed | tf_op | source)
XLA Modules:
  0.0 21.5 jit_solution(13563117491794912578)
XLA Ops:
  0.6 1.3 %faces.1 = (bf16[8,64,128]{2,1,0:T(8,128)(2,1)S(1)}, bf16[8,64,512]{2,1,0:T(8,128)(2,1)S(1)}, s32[8,512]{1,0:T(8,128)S(1)}, f32[1,64]{1,0:T(1,128)S(1)}, f32[1,6...) custom-call(bf16[8,64,512]{2,1,0:T(8,128)(2,1)} %refs_0_.1, ...), custom_call_target="tpu_custom_call" | custom-call | tf_op jit(solution)/shard_map/faces/pallas_call | solution.py:384
  1.9 3.8 %collective-permute-start.1 = (bf16[8,64,128]{2,1,0:T(8,128)(2,1)S(1)}, bf16[8,64,128]{2,1,0:T(8,128)(2,1)S(1)}, u32[]{:S(2)}, u32[]{:S(2)}) collective-permute-start(bf16[8,64,128]{2,1,0:T(8,128)(2,1)S(1)} %get-tuple-element.21), channel_id=1, source_target_pairs={{1,2},{3,4},{5,6},{7,8},{9,10},{11,12},{13,14},{15,16},{17,18},{19... | collective-permute-start | bytes 393224 | tf_op jit(solution)/shard_map/ppermute | solution.py:398
  5.7 6.9 %collective-permute-start = (bf16[8,64,128]{2,1,0:T(8,128)(2,1)S(1)}, bf16[8,64,128]{2,1,0:T(8,128)(2,1)S(1)}, u32[]{:S(2)}, u32[]{:S(2)}) collective-permute-start(bf16[8,64,128]{2,1,0:T(8,128)(2,1)S(1)} %get-tuple-element.21), channel_id=1, source_target_pairs={{0,1},{1,0},{2,3},{3,2},{4,5},{5,4},{6,7},{7,6},{8,9},{9,8},{10,11... | collective-permute-start | bytes 393224 | tf_op jit(solution)/shard_map/ppermute | solution.py:396
  12.6 0.0 copy-start
  12.6 0.0 copy-start.1
  12.6 0.0 copy-start.2
  12.6 0.0 copy-start.3
  12.6 3.6 %inner.1.base_ref = f32[8,64,512]{2,1,0:T(8,128)S(1)} custom-call(s32[8,26]{1,0:T(8,128)S(1)} %get-tuple-element.14.nb_ref, bf16[8,64,512]{2,1,0:T(8,128)(2,1)S(1)} %get-tuple-element.16.features_ref, s32[8,512]{1,0:T(8,128)S(1)} %get-tuple-element.17.occ_ref, f32[1,64]{1,0:T(1,128)S(1)} %get-tuple-element.18.gain_ref, ...), custom_call_target="tpu_custom_call" | custom-call | flops 905969664 | bytes 2097152 | tf_op jit(solution)/shard_map/inner/pallas_call | solution.py:400
  16.2 0.0 collective-permute-done.1.far_ref
  16.3 0.0 collective-permute-done.chip_ref
  16.3 0.0 copy-done
  16.3 0.0 copy-done.1
  16.3 0.0 copy-done.2
  16.3 0.0 copy-done.3
  16.3 3.1 %outer.1 = (bf16[8,64,512]{2,1,0:T(8,128)(2,1)}, bf16[128,512]{1,0:T(8,128)(2,1)S(1)}, bf16[128,512]{1,0:T(8,128)(2,1)S(1)}) custom-call(s32[8,26]{1,0:T(8,128)S(1)} %get-tuple-element.14.nb_ref, s32[1,8]{1,0:T(1,128)S(1)} %get-tuple-element.15.map_ref, f32[8,64,512]{2,1,0:T(8,128)S(1)} %inner.1.base_ref, ...), custom_call_target="tpu_custom_call" | custom-call | tf_op jit(solution)/shard_map/outer/pallas_call | solution.py:421
  19.4 0.1 collective-permute-start.2
  19.6 1.3 %collective-permute-done.2 = bf16[128,512]{1,0:T(8,128)(2,1)S(1)} collective-permute-done((bf16[128,512]{1,0:T(8,128)(2,1)S(1)}, bf16[128,512]{1,0:T(8,128)(2,1)S(1)}, u32[]{:S(2)}, u32[]{:S(2)}) %collective-permute-start.2) | collective-permute-done | bytes 131104 | tf_op jit(solution)/shard_map/ppermute | solution.py:460
  20.9 0.7 %add_bitcast_fusion = bf16[1,128,512]{2,1,0:T(8,128)(2,1)} fusion(bf16[128,512]{1,0:T(8,128)(2,1)S(1)} %get-tuple-element.24, bf16[128,512]{1,0:T(8,128)(2,1)S(1)} %collective-permute-done.2), kind=kLoop, calls=%fused_computation | loop fusion | flops 65536 | bytes 393216 | tf_op jit(solution)/shard_map/broadcast_in_dim | solution.py:461
Async XLA Ops:
  1.9 14.3 %collective-permute-start.1 = (bf16[8,64,128]{2,1,0:T(8,128)(2,1)S(1)}, bf16[8,64,128]{2,1,0:T(8,128)(2,1)S(1)}, u32[]{:S(2)}, u32[]{:S(2)}) collective-permute-start(bf16[8,64,128]{2,1,0:T(8,128)(2,1)S(1)} %get-tuple-element.21), channel_id=1, source_target_pairs={{1,2},{3,4},{5,6},{7,8},{9,10},{11,12},{13,14},{15,16},{17,18},{19... | collective-permute-start | bytes 393224 | tf_op jit(solution)/shard_map/ppermute | solution.py:398
  5.7 10.5 %collective-permute-start = (bf16[8,64,128]{2,1,0:T(8,128)(2,1)S(1)}, bf16[8,64,128]{2,1,0:T(8,128)(2,1)S(1)}, u32[]{:S(2)}, u32[]{:S(2)}) collective-permute-start(bf16[8,64,128]{2,1,0:T(8,128)(2,1)S(1)} %get-tuple-element.21), channel_id=1, source_target_pairs={{0,1},{1,0},{2,3},{3,2},{4,5},{5,4},{6,7},{7,6},{8,9},{9,8},{10,11... | collective-permute-start | bytes 393224 | tf_op jit(solution)/shard_map/ppermute | solution.py:396
  12.6 3.6 %copy-start = (bf16[2,512,512]{2,1,0:T(8,128)(2,1)S(1)}, bf16[2,512,512]{2,1,0:T(8,128)(2,1)}, u32[]{:S(2)}) copy-start(bf16[2,512,512]{2,1,0:T(8,128)(2,1)} %constant.6.clone.sort_ref) | copy-start | bytes 3145732
  12.6 3.6 %copy-start.1 = (bf16[8,64,128]{2,1,0:T(8,128)(2,1)S(1)}, bf16[8,64,128]{2,1,0:T(8,128)(2,1)}, u32[]{:S(2)}) copy-start(bf16[8,64,128]{2,1,0:T(8,128)(2,1)} %stride_ref.1) | copy-start | bytes 393220
  12.6 3.7 %copy-start.2 = (bf16[64,512]{1,0:T(8,128)(2,1)S(1)}, bf16[64,512]{1,0:T(8,128)(2,1)}, u32[]{:S(2)}) copy-start(bf16[64,512]{1,0:T(8,128)(2,1)} %constant.7.clone.entry_ref) | copy-start | bytes 196612
  12.6 3.7 %copy-start.3 = (f32[8,1,512]{2,1,0:T(1,128)S(1)}, f32[8,1,512]{2,1,0:T(1,128)}, u32[]{:S(2)}) copy-start(f32[8,1,512]{2,1,0:T(1,128)} %constant.8.clone.place_ref) | copy-start | bytes 49156
  19.4 1.4 %collective-permute-start.2 = (bf16[128,512]{1,0:T(8,128)(2,1)S(1)}, bf16[128,512]{1,0:T(8,128)(2,1)S(1)}, u32[]{:S(2)}, u32[]{:S(2)}) collective-permute-start(bf16[128,512]{1,0:T(8,128)(2,1)S(1)} %get-tuple-element.25), channel_id=1, source_target_pairs={{0,1},{1,0},{2,3},{3,2},{4,5},{5,4},{6,7},{7,6},{8,9},{9,8},{10,11... | collective-permute-start | bytes 393224 | tf_op jit(solution)/shard_map/ppermute | solution.py:460

commit v4 on v3

--- a/solution.py
+++ b/solution.py
@@ -1,3 +1,5 @@
+import functools
+
 import jax
 import jax.numpy as jnp
 import ml_dtypes
@@ -17,7 +19,8 @@
 LANES = 128
 TAPS = 9
 
-LOADED = range(8)
+LOADED = 8
+HALF = BRK // 2
 
 ROLLS = (0, 64, 8, 120, 72, 56)
 PLAIN, SWAP, UP, DOWN, SWAP_UP, SWAP_DOWN = range(6)
@@ -112,7 +115,7 @@
 
 
 def faces_kernel(*refs):
-    count = len(LOADED)
+    count = LOADED
     sources, face_ref, kept, sems = refs[:count], refs[count], refs[count + 1 : -1], refs[-1]
     copies = [
         pltpu.make_async_copy(source, target, sems.at[k])
@@ -136,8 +139,8 @@
 
 
 def inner_kernel(
-    nb_ref, features_ref, occ_ref, gain_ref, shift_ref, weight_ref, base_ref,
-    acts, wide, stack, ybuf, nb, sem,
+    nb_ref, features_ref, occ_ref, gain_ref, shift_ref, weight_ref, edge_ref, middle_ref, wide,
+    acts, stack, ybuf, nb, sem,
 ):
     copy = pltpu.make_async_copy(nb_ref, nb, sem)
     copy.start()
@@ -183,7 +186,11 @@
                 to_low = to_low + y[2 * CH :, columns(j + 1)]
             moved = pltpu.roll(jnp.where(low, to_low, to_high), 64, 1)
             total = y[CH : 2 * CH, columns(j)] + features_ref[i, :, columns(j)].astype(F32)
-            base_ref[i, :, columns(j)] = (total + shift) + moved
+            total = occ_ref[i : i + 1, columns(j)].astype(F32) * ((total + shift) + moved)
+            if j in (0, 3):
+                edge_ref[i, :, columns(j // 3)] = total
+            else:
+                middle_ref[i, :, columns(j - 1)] = total.astype(BF)
 
     waiting = None
     for i in range(BRK + 1):
@@ -217,11 +224,37 @@
                 finish(i - 1, 1)
 
 
+def sorted_voxels(rows, sort_ref, picked, low):
+    sorted_ = [
+        jnp.dot(
+            jnp.concatenate([rows[k], rows[2 + k]], axis=0),
+            sort_ref[k],
+            preferred_element_type=F32,
+        ).astype(BF)
+        for k in range(2)
+    ]
+    for pair in range(2):
+        part = slice(pair * CH, (pair + 1) * CH)
+        for j in range(4):
+            one, two = sorted_[0][part, columns(j)], sorted_[1][part, columns(j)]
+            taps = slice(j * CH, (j + 1) * CH)
+            picked[0, taps, columns(pair)] = jnp.where(low, one, two)
+            picked[1, taps, columns(pair)] = jnp.where(low, two, one)
+
+
+def octants(wide2, picked, bias):
+    even, odd = (jnp.dot(wide2[c], picked[c], preferred_element_type=F32) for c in range(2))
+    both = [
+        even[:, columns(pair)] + pltpu.roll(odd[:, columns(pair)], 64, 1) for pair in range(2)
+    ]
+    return (jnp.concatenate(both, axis=1) + bias).astype(BF)
+
+
 def outer_kernel(
-    nb_ref, map_ref, base_ref, chip_ref, far_ref, occ_ref, weight_ref, stride_ref, bias_ref,
+    nb_ref, map_ref, edge_ref, middle_ref, chip_ref, far_ref, occ_ref, wide, stride_ref, bias_ref,
     sort_ref, entry_ref, place_ref,
-    fine_hbm, stay_ref, leave_ref,
-    fine_ref, halo, wide, wide2, stack, picked, placing, mask, nb, map_, order, sems,
+    ends_ref, rows_ref, placing_ref, wide2, leave_ref,
+    halo, stack, picked, placing, mask, faces, leaving_ends, nb, map_, order, sems,
 ):
     copies = [
         pltpu.make_async_copy(nb_ref, nb, sems.at[0]),
@@ -238,20 +271,19 @@
     for i in range(BRK):
         halo[odd, i] = chip_ref[i]
         halo[1 - odd, i] = far_ref[i]
-    for i in range(BRK):
-        mask[i] = occ_ref[i : i + 1, :].astype(F32)
+        row = slice(i, i + 1)
+        mask[i] = jnp.where(
+            low32[:1], occ_ref[row, columns(0)], occ_ref[row, columns(3)]
+        ).astype(F32)
     halo[0, BRK] = jnp.zeros((CH, LANES), BF)
     halo[1, BRK] = jnp.zeros((CH, LANES), BF)
-    for row, a in enumerate((0, 2)):
-        wide[row * CH : (row + 1) * CH, :] = (
-            weight_ref[TAPS * a : TAPS * (a + 1)].reshape(TAPS * CH, CH).T
-        )
     for c in range(2):
         taps = jnp.concatenate([stride_ref[2 * k + c] for k in range(4)], axis=0)
         wide2[c] = taps.T
+    bias = column(bias_ref[...])
     for copy in copies:
         copy.wait()
-    staying, leaving = jnp.int32(0), jnp.int32(BRK // 2)
+    leaving, staying = jnp.int32(0), jnp.int32(HALF)
     for i in range(BRK):
         stays = (map_[0, i] >> 3) == device
         order[jnp.where(stays, staying, leaving)] = i
@@ -269,44 +301,35 @@
 
         return raw
 
-    def finish(pair):
+    def product(pair):
         lanes = slice(2 * pair * LANES, 2 * (pair + 1) * LANES)
-        edge = jnp.dot(wide[...], stack[:, lanes], preferred_element_type=F32)
-        for k in range(2):
-            i = brick[2 * pair + k]
-            mine = edge[:, columns(k)]
-            moved = pltpu.roll(jnp.where(low32, mine[CH:], mine[:CH]), 64, 1)
-            for j in range(4):
-                total = base_ref[i, :, columns(j)]
-                if j == 0:
-                    total = total + jnp.where(low32, moved, 0.0)
-                if j == 3:
-                    total = total + jnp.where(low32, 0.0, moved)
-                occupied = mask[i, :, columns(j)]
-                fine_ref[i, :, columns(j)] = (occupied * total).astype(BF)
-
-    def sort(half):
-        sorted_ = []
-        for k in range(2):
-            rows = [fine_ref[brick[4 * half + 2 * pair + k]] for pair in range(2)]
-            sorted_.append(
-                jnp.dot(
-                    jnp.concatenate(rows, axis=0), sort_ref[k], preferred_element_type=F32
-                ).astype(BF)
-            )
-        for pair in range(2):
-            rows = slice(pair * CH, (pair + 1) * CH)
-            for j in range(4):
-                one, two = sorted_[0][rows, columns(j)], sorted_[1][rows, columns(j)]
-                taps = slice(j * CH, (j + 1) * CH)
-                picked[0, taps, columns(2 * half + pair)] = jnp.where(low, one, two)
-                picked[1, taps, columns(2 * half + pair)] = jnp.where(low, two, one)
-
-    for k in range(BRK):
+        ends = jnp.concatenate([wide[:CH], wide[2 * CH :]], axis=0)
+        faces[:, lanes] = jnp.dot(ends, stack[:, lanes], preferred_element_type=F32)
+
+    def finish(k):
+        i = brick[k]
+        mine = faces[:, columns(k)]
+        moved = pltpu.roll(jnp.where(low32, mine[CH:], mine[:CH]), 64, 1) * mask[i]
+        for side in range(2):
+            keep = low32 if side == 0 else jnp.logical_not(low32)
+            fine = (edge_ref[i, :, columns(side)] + jnp.where(keep, moved, 0.0)).astype(BF)
+            ends_ref[i, :, columns(side)] = fine
+            if k < HALF:
+                leaving_ends[k, :, columns(side)] = fine
+            else:
+                rows_ref[k - HALF, :, columns(2 + side)] = fine
+        if k >= HALF:
+            rows_ref[k - HALF, :, : 2 * LANES] = middle_ref[i]
+
+    def place(k, target):
         which = map_[0, brick[k]] & 7
-        row = place_ref[which].astype(BF)
-        placing[k * CH : (k + 1) * CH, :] = entry_ref[...] * row
-    first, second = None, None
+        part = slice(k % HALF * CH, (k % HALF + 1) * CH)
+        target[part, :] = entry_ref[...] * place_ref[which].astype(BF)
+
+    for k in range(HALF):
+        place(k, placing)
+        place(HALF + k, placing_ref)
+    first, second, result = None, None, None
     for k in range(BRK + 2):
         now = halo_stage(raw_of(brick[k]), masks) if k < BRK else None
         later = halo_second(first, masks) if first is not None else None
@@ -317,37 +340,57 @@
                 stack[tap * CH : (tap + 1) * CH, columns(spot)] = piece
 
             second_stage(second, masks, store)
+            if spot == 2 or spot == 4 or spot == 6:
+                finish(spot - 2)
+                finish(spot - 1)
             if spot % 2 == 1:
-                finish(spot // 2)
-                if spot == 5:
-                    sort(0)
+                product(spot // 2)
+            if spot == 5:
+                rows = [
+                    jnp.concatenate([middle_ref[brick[q]], leaving_ends[q]], axis=1)
+                    for q in range(HALF)
+                ]
+                sorted_voxels(rows, sort_ref, picked, low)
+            if spot == 6:
+                result = octants(wide2, picked, bias)
+            if spot == 7:
+                leave_ref[...] = jnp.dot(
+                    result, placing[...], preferred_element_type=F32
+                ).astype(BF)
         first, second = now, later
-    out = pltpu.make_async_copy(fine_ref, fine_hbm, sems.at[2])
-    out.start()
-    sort(1)
-    octant = []
-    for pair in range(BRK // 2):
-        even, odd = (
-            jnp.dot(wide2[c], picked[c, :, columns(pair)], preferred_element_type=F32)
-            for c in range(2)
+    finish(BRK - 2)
+    finish(BRK - 1)
+
+
+def staying_kernel(
+    ends_ref, middle_ref, rows_ref, placing_ref, wide2, sort_ref, bias_ref,
+    fine_hbm, stay_ref, picked, sems,
+):
+    copies = [
+        pltpu.make_async_copy(middle_ref, fine_hbm.at[:, :, LANES : 3 * LANES], sems.at[0])
+    ] + [
+        pltpu.make_async_copy(
+            ends_ref.at[:, :, columns(side)], fine_hbm.at[:, :, columns(3 * side)], sems.at[1 + side]
         )
-        octant.append(even + pltpu.roll(odd, 64, 1))
-    octant = (jnp.concatenate(octant, axis=1) + column(bias_ref[...])).astype(BF)
-    half = BRK // 2 * CH
-    leave_ref[...] = jnp.dot(
-        octant[:, half:], placing[half:, :], preferred_element_type=F32
-    ).astype(BF)
-    stay_ref[...] = jnp.dot(
-        octant[:, :half], placing[:half, :], preferred_element_type=F32
-    ).astype(BF)
-    out.wait()
+        for side in range(2)
+    ]
+    for copy in copies:
+        copy.start()
+    low = lane_masks()[4]
+    sorted_voxels([rows_ref[k] for k in range(HALF)], sort_ref, picked, low)
+    octant = octants(wide2, picked, column(bias_ref[...]))
+    stay_ref[...] = jnp.dot(octant, placing_ref[...], preferred_element_type=F32).astype(BF)
+    for copy in copies:
+        copy.wait()
 
 
 def tables():
     voxel = np.arange(VOX)
     x, y, z = voxel >> 6, (voxel >> 3) & 7, voxel & 7
     lane = 64 * (4 * (x & 1) + 2 * (y & 1) + (z & 1)) + 16 * (x >> 1) + 4 * (y >> 1) + (z >> 1)
-    sort = np.stack([lane[:, None] == voxel, (lane ^ 64)[:, None] == voxel]).astype(ml_dtypes.bfloat16)
+    sort = np.stack([lane[:, None] == voxel, (lane ^ 64)[:, None] == voxel])
+    sort = sort.reshape(2, 4, LANES, VOX)[:, [1, 2, 0, 3]].reshape(2, VOX, VOX)
+    sort = sort.astype(ml_dtypes.bfloat16)
     source = 16 * (x & 3) + 4 * (y & 3) + (z & 3)
     entry = (np.arange(64)[:, None] == source[None, :]).astype(ml_dtypes.bfloat16)
     octant = 4 * (x >> 2) + 2 * (y >> 2) + (z >> 2)
@@ -397,14 +440,17 @@
     across = [(i, i + 1) for i in range(1, total - 1, 2)]
     far = lax.ppermute(face, ("bricks", "grp"), across + [(j, i) for i, j in across])
 
-    base = pl.pallas_call(
+    edge, middle, wide = pl.pallas_call(
         inner_kernel,
         in_specs=[vmem] * 6,
-        out_specs=vmem,
-        out_shape=jax.ShapeDtypeStruct((BRK, CH, VOX), F32),
+        out_specs=[vmem] * 3,
+        out_shape=(
+            jax.ShapeDtypeStruct((BRK, CH, 2 * LANES), F32),
+            jax.ShapeDtypeStruct((BRK, CH, 2 * LANES), BF),
+            jax.ShapeDtypeStruct((3 * CH, TAPS * CH), BF),
+        ),
         scratch_shapes=[
             pltpu.VMEM((len(ROLLS), BRK + 1, CH, VOX), BF),
-            pltpu.VMEM((3 * CH, TAPS * CH), BF),
             pltpu.VMEM((2, TAPS * CH, VOX), BF),
             pltpu.VMEM((2, 3 * CH, VOX), F32),
             pltpu.SMEM((BRK, 26), jnp.int32),
@@ -418,39 +464,42 @@
     )(neighbours, features, occupancy, gain, shift, conv_weight)
 
     sort, entry, place = (jnp.asarray(table) for table in tables())
-    fine, stay, leave = pl.pallas_call(
+    placed = jax.ShapeDtypeStruct((CH2, VOX), BF)
+    ends, rows, placing, wide2, leave = pl.pallas_call(
         outer_kernel,
-        in_specs=[vmem] * 12,
-        out_specs=[pl.BlockSpec(memory_space=pltpu.HBM), vmem, vmem],
+        in_specs=[vmem] * 13,
+        out_specs=[vmem] * 5,
         out_shape=(
-            jax.ShapeDtypeStruct((BRK, CH, VOX), BF),
-            jax.ShapeDtypeStruct((CH2, VOX), BF),
-            jax.ShapeDtypeStruct((CH2, VOX), BF),
+            jax.ShapeDtypeStruct((BRK, CH, 2 * LANES), BF),
+            jax.ShapeDtypeStruct((HALF, CH, VOX), BF),
+            jax.ShapeDtypeStruct((HALF * CH, VOX), BF),
+            jax.ShapeDtypeStruct((2, CH2, 4 * CH), BF),
+            placed,
         ),
         scratch_shapes=[
-            pltpu.VMEM((BRK, CH, VOX), BF),
             pltpu.VMEM((2, BRK + 1, CH, LANES), BF),
-            pltpu.VMEM((2 * CH, TAPS * CH), BF),
-            pltpu.VMEM((2, CH2, 4 * CH), BF),
             pltpu.VMEM((TAPS * CH, BRK * LANES), BF),
-            pltpu.VMEM((2, 4 * CH, BRK * CH), BF),
-            pltpu.VMEM((BRK * CH, VOX), BF),
-            pltpu.VMEM((BRK, 1, VOX), F32),
+            pltpu.VMEM((2, 4 * CH, HALF * CH), BF),
+            pltpu.VMEM((HALF * CH, VOX), BF),
+            pltpu.VMEM((BRK, 1, LANES), F32),
+            pltpu.VMEM((2 * CH, BRK * LANES), F32),
+            pltpu.VMEM((HALF, CH, 2 * LANES), BF),
             pltpu.SMEM((BRK, 26), jnp.int32),
             pltpu.SMEM((1, BRK), jnp.int32),
             pltpu.SMEM((BRK,), jnp.int32),
-            pltpu.SemaphoreType.DMA((3,)),
+            pltpu.SemaphoreType.DMA((2,)),
         ],
         compiler_params=pltpu.CompilerParams(vmem_limit_bytes=16 << 20),
         name="outer",
     )(
         neighbours,
         coarse_map,
-        base,
+        edge,
+        middle,
         chip,
         far,
         occupancy,
-        conv_weight,
+        wide,
         stride_weight,
         bias,
         sort,
@@ -458,6 +507,21 @@
         place,
     )
     arrived = lax.ppermute(leave, "grp", [(i, i ^ 1) for i in range(groups)])
+    fine, stay = pl.pallas_call(
+        staying_kernel,
+        in_specs=[vmem] * 7,
+        out_specs=[pl.BlockSpec(memory_space=pltpu.HBM), vmem],
+        out_shape=(jax.ShapeDtypeStruct((BRK, CH, VOX), BF), placed),
+        scratch_shapes=[
+            pltpu.VMEM((2, 4 * CH, HALF * CH), BF),
+            pltpu.SemaphoreType.DMA((3,)),
+        ],
+        compiler_params=pltpu.CompilerParams(vmem_limit_bytes=8 << 20),
+        cost_estimate=pl.CostEstimate(
+            flops=2 * 8 * CH * CH2 * VOX * HALF, bytes_accessed=2 << 20, transcendentals=0
+        ),
+        name="staying",
+    )(ends, middle, rows, placing, wide2, sort, bias)
     return fine, (stay + arrived)[None]
 
 

time: 21.6 us -> 20.9 us (0.968)
  waiting for transfers between devices: 1.3 us -> 0.44 us
    ppermute x1, waiting for transfers between devices: 1.3 us -> 0.43 us  [shards(): arrived = lax.ppermute(leave, 'grp', [(i, i ^ 1) for i in range(groups)])]
    pallas_call x2 -> x3, Pallas kernels: 6.7 us -> 6.82 us  [the longest x1 3.71 us: shards(): pl.pallas_call(inner_kernel, in_specs=[vmem] * 6, out_specs=[vmem] * 3, o...]
  transfers between devices with their start and end apart: 3 -> 3, of which waited for: 1 -> 1; matrix products, arithmetic and copies ran while one was open for 0% -> 0% of each run, Pallas kernels for 17% -> 22%
where the time goes in v4:
time: 20.9 us; the launch traced here: 20.8 us
  starting transfers between devices  10.8 us (52%)
  Pallas kernels  8.12 us (39%)
  between operations  0.73 us (3%)
  other arithmetic  0.67 us (3%)
  waiting for transfers between devices  0.44 us (2%)
    ppermute x1, starting transfers between devices, shards(): chip = lax.ppermute(face, 'grp', [(i, i ^ 1) for i in range(groups)])  6.92 us
    ppermute x1, starting transfers between devices, shards(): lax.ppermute(face, ('bricks', 'grp'), across + [(j, i) for i, j in across])  3.77 us
    pallas_call x1, Pallas kernels, shards(): pl.pallas_call(inner_kernel, in_specs=[vmem] * 6, out_specs=[vmem] * 3, o...  3.71 us
    pallas_call x1, Pallas kernels, shards(): pl.pallas_call(outer_kernel, in_specs=[vmem] * 13, out_specs=[vmem] * 5,...  2.25 us
    pallas_call x1, Pallas kernels, shards(): pl.pallas_call(faces_kernel, in_specs=[pl.BlockSpec(memory_space=pltpu.HB...  1.3 us
    pallas_call x1, Pallas kernels, shards(): pl.pallas_call(staying_kernel, in_specs=[vmem] * 7, out_specs=[pl.BlockSp...  0.86 us
    broadcast_in_dim x1, other arithmetic, shards(): return (fine, (stay + arrived)[None])  0.67 us
    ppermute x1, waiting for transfers between devices, shards(): arrived = lax.ppermute(leave, 'grp', [(i, i ^ 1) for i in range(groups)])  0.43 us
  transfers between devices with their start and end apart: 3, of which 1 were waited for; matrix products, arithmetic and copies ran while one was open for 0% of the time, Pallas kernels for 22%

profile of v4, /device:TPU:7, one launch (start us, length us, event | category | flops | bytes accessed | tf_op | source)
XLA Modules:
  0.0 20.8 jit_solution(15649314501401061958)
XLA Ops:
  0.6 1.3 %faces.1 = (bf16[8,64,128]{2,1,0:T(8,128)(2,1)S(1)}, bf16[8,64,512]{2,1,0:T(8,128)(2,1)S(1)}, s32[8,512]{1,0:T(8,128)S(1)}, f32[1,64]{1,0:T(1,128)S(1)}, f32[1,6...) custom-call(bf16[8,64,512]{2,1,0:T(8,128)(2,1)} %refs_0_.1, ...), custom_call_target="tpu_custom_call" | custom-call | tf_op jit(solution)/shard_map/faces/pallas_call | solution.py:427
  1.9 3.8 %collective-permute-start.1 = (bf16[8,64,128]{2,1,0:T(8,128)(2,1)S(1)}, bf16[8,64,128]{2,1,0:T(8,128)(2,1)S(1)}, u32[]{:S(2)}, u32[]{:S(2)}) collective-permute-start(bf16[8,64,128]{2,1,0:T(8,128)(2,1)S(1)} %get-tuple-element.30), channel_id=1, source_target_pairs={{1,2},{3,4},{5,6},{7,8},{9,10},{11,12},{13,14},{15,16},{17,18},{19... | collective-permute-start | bytes 393224 | tf_op jit(solution)/shard_map/ppermute | solution.py:441
  5.7 6.9 %collective-permute-start = (bf16[8,64,128]{2,1,0:T(8,128)(2,1)S(1)}, bf16[8,64,128]{2,1,0:T(8,128)(2,1)S(1)}, u32[]{:S(2)}, u32[]{:S(2)}) collective-permute-start(bf16[8,64,128]{2,1,0:T(8,128)(2,1)S(1)} %get-tuple-element.30), channel_id=1, source_target_pairs={{0,1},{1,0},{2,3},{3,2},{4,5},{5,4},{6,7},{7,6},{8,9},{9,8},{10,11... | collective-permute-start | bytes 393224 | tf_op jit(solution)/shard_map/ppermute | solution.py:439
  12.6 0.0 copy-start
  12.6 0.0 copy-start.1
  12.6 0.0 copy-start.2
  12.6 0.0 copy-start.3
  12.6 3.7 %inner.1 = (f32[8,64,256]{2,1,0:T(8,128)S(1)}, bf16[8,64,256]{2,1,0:T(8,128)(2,1)S(1)}, bf16[192,576]{1,0:T(8,128)(2,1)S(1)}) custom-call(s32[8,26]{1,0:T(8,128)S(1)} %get-tuple-element.21.nb_ref, bf16[8,64,512]{2,1,0:T(8,128)(2,1)S(1)} %get-tuple-element.23.features_ref, s32[8,512]{1,0:T(8,128)S(1)} %get-tuple-element.24.occ_ref, ...), custom_call_target="tpu_custom_call" | custom-call | flops 905969664 | bytes 2097152 | tf_op jit(solution)/shard_map/inner/pallas_call | solution.py:443
  16.4 0.0 collective-permute-done.1.far_ref
  16.4 0.0 collective-permute-done.chip_ref
  16.4 0.0 copy-done
  16.4 0.0 copy-done.1
  16.4 0.0 copy-done.2
  16.4 0.0 copy-done.3
  16.4 2.2 %outer.1 = (bf16[8,64,256]{2,1,0:T(8,128)(2,1)S(1)}, bf16[4,64,512]{2,1,0:T(8,128)(2,1)S(1)}, bf16[256,512]{1,0:T(8,128)(2,1)S(1)}, bf16[2,128,256]{2,1,0:T(8,128)(2,1)S(1)}, bf16[128,512]{1,0:T(8,128)(2,1)S(1)}) custom-call(s32[8,26]{1,0:T(8,128)S(1)} %get-tuple-element.21.nb_ref, s32[1,8]{1,0:T(1,128)S(1)} %get-tuple-element.22.map_ref, ...), custom_call_target="tpu_custom_call" | custom-call | tf_op jit(solution)/shard_map/outer/pallas_call | solution.py:468
  18.7 0.1 collective-permute-start.2
  18.8 0.9 %staying.1 = (bf16[8,64,512]{2,1,0:T(8,128)(2,1)}, bf16[128,512]{1,0:T(8,128)(2,1)S(1)}) custom-call(bf16[8,64,256]{2,1,0:T(8,128)(2,1)S(1)} %get-tuple-element.33.ends_ref, bf16[8,64,256]{2,1,0:T(8,128)(2,1)S(1)} %get-tuple-element.29.middle_ref, bf16[4,64,512]{2,1,0:T(8,128)(2,1)S(1)} %get-tuple-element.34.rows_ref, ...), custom_call_target="tpu_custom_call" | custom-call | flops 268435456 | bytes 2097152 | tf_op jit(solution)/shard_map/staying/pallas_call | solution.py:510
  19.7 0.4 %collective-permute-done.2 = bf16[128,512]{1,0:T(8,128)(2,1)S(1)} collective-permute-done((bf16[128,512]{1,0:T(8,128)(2,1)S(1)}, bf16[128,512]{1,0:T(8,128)(2,1)S(1)}, u32[]{:S(2)}, u32[]{:S(2)}) %collective-permute-start.2) | collective-permute-done | bytes 131104 | tf_op jit(solution)/shard_map/ppermute | solution.py:509
  20.1 0.7 %add_bitcast_fusion = bf16[1,128,512]{2,1,0:T(8,128)(2,1)} fusion(bf16[128,512]{1,0:T(8,128)(2,1)S(1)} %get-tuple-element.38, bf16[128,512]{1,0:T(8,128)(2,1)S(1)} %collective-permute-done.2), kind=kLoop, calls=%fused_computation | loop fusion | flops 65536 | bytes 393216 | tf_op jit(solution)/shard_map/broadcast_in_dim | solution.py:525
Async XLA Ops:
  1.9 14.4 %collective-permute-start.1 = (bf16[8,64,128]{2,1,0:T(8,128)(2,1)S(1)}, bf16[8,64,128]{2,1,0:T(8,128)(2,1)S(1)}, u32[]{:S(2)}, u32[]{:S(2)}) collective-permute-start(bf16[8,64,128]{2,1,0:T(8,128)(2,1)S(1)} %get-tuple-element.30), channel_id=1, source_target_pairs={{1,2},{3,4},{5,6},{7,8},{9,10},{11,12},{13,14},{15,16},{17,18},{19... | collective-permute-start | bytes 393224 | tf_op jit(solution)/shard_map/ppermute | solution.py:441
  5.7 10.7 %collective-permute-start = (bf16[8,64,128]{2,1,0:T(8,128)(2,1)S(1)}, bf16[8,64,128]{2,1,0:T(8,128)(2,1)S(1)}, u32[]{:S(2)}, u32[]{:S(2)}) collective-permute-start(bf16[8,64,128]{2,1,0:T(8,128)(2,1)S(1)} %get-tuple-element.30), channel_id=1, source_target_pairs={{0,1},{1,0},{2,3},{3,2},{4,5},{5,4},{6,7},{7,6},{8,9},{9,8},{10,11... | collective-permute-start | bytes 393224 | tf_op jit(solution)/shard_map/ppermute | solution.py:439
  12.6 3.8 %copy-start = (bf16[2,512,512]{2,1,0:T(8,128)(2,1)S(1)}, bf16[2,512,512]{2,1,0:T(8,128)(2,1)}, u32[]{:S(2)}) copy-start(bf16[2,512,512]{2,1,0:T(8,128)(2,1)} %constant.6.clone.sort_ref) | copy-start | bytes 3145732
  12.6 3.8 %copy-start.1 = (bf16[8,64,128]{2,1,0:T(8,128)(2,1)S(1)}, bf16[8,64,128]{2,1,0:T(8,128)(2,1)}, u32[]{:S(2)}) copy-start(bf16[8,64,128]{2,1,0:T(8,128)(2,1)} %stride_ref.1) | copy-start | bytes 393220
  12.6 3.8 %copy-start.2 = (bf16[64,512]{1,0:T(8,128)(2,1)S(1)}, bf16[64,512]{1,0:T(8,128)(2,1)}, u32[]{:S(2)}) copy-start(bf16[64,512]{1,0:T(8,128)(2,1)} %constant.7.clone.entry_ref) | copy-start | bytes 196612
  12.6 3.8 %copy-start.3 = (f32[8,1,512]{2,1,0:T(1,128)S(1)}, f32[8,1,512]{2,1,0:T(1,128)}, u32[]{:S(2)}) copy-start(f32[8,1,512]{2,1,0:T(1,128)} %constant.8.clone.place_ref) | copy-start | bytes 49156
  18.7 1.4 %collective-permute-start.2 = (bf16[128,512]{1,0:T(8,128)(2,1)S(1)}, bf16[128,512]{1,0:T(8,128)(2,1)S(1)}, u32[]{:S(2)}, u32[]{:S(2)}) collective-permute-start(bf16[128,512]{1,0:T(8,128)(2,1)S(1)} %get-tuple-element.39), channel_id=1, source_target_pairs={{0,1},{1,0},{2,3},{3,2},{4,5},{5,4},{6,7},{7,6},{8,9},{9,8},{10,11... | collective-permute-start | bytes 393224 | tf_op jit(solution)/shard_map/ppermute | solution.py:509

commit v5 on v4

--- a/solution.py
+++ b/solution.py
@@ -53,61 +53,47 @@
     lane = lax.broadcasted_iota(jnp.int32, (CH, LANES), 1)
     z = lane & 7
     y = (lane >> 3) & 7
-    return z == 0, z == 7, y == 0, y == 7, lane < 64
-
-
-def first_stage(take, masks):
-    z0, z7, y0, y7, _ = masks
+    return (z == 0, z == 7), {row: y == row for row in (0, 1, 6, 7)}, lane < 64
+
+
+def merged(take, masks):
+    (z0, z7), y, _ = masks
     centre = take(PLAIN, 0, 0)
-    edge = jnp.where(y0, take(SWAP, 1, 0), take(SWAP, -1, 0))
-    edge_up = jnp.where(y0, take(SWAP_UP, -1, 1), take(SWAP_UP, 1, 1))
-    edge_down = jnp.where(y7, take(SWAP_DOWN, 1, -1), take(SWAP_DOWN, -1, -1))
-    middle = (
-        pltpu.roll(jnp.where(z7, take(DOWN, 0, -1), centre), 1, 1),
+    up, down = take(UP, 0, 1), take(DOWN, 0, -1)
+    above = jnp.where(y[0], take(SWAP, 1, 0), centre)
+    below = jnp.where(y[7], take(SWAP, -1, 0), centre)
+    return (
+        jnp.where(z7, jnp.where(y[6], take(SWAP_DOWN, -1, -1), down), below),
+        below,
+        jnp.where(z0, jnp.where(y[0], take(SWAP_UP, -1, 1), up), below),
+        jnp.where(z7, down, centre),
         centre,
-        pltpu.roll(jnp.where(z0, take(UP, 0, 1), centre), 127, 1),
+        jnp.where(z0, up, centre),
+        jnp.where(z7, jnp.where(y[7], take(SWAP_DOWN, 1, -1), down), above),
+        above,
+        jnp.where(z0, jnp.where(y[1], take(SWAP_UP, 1, 1), up), above),
     )
-    edges = (
-        pltpu.roll(jnp.where(z7, edge_down, edge), 1, 1),
-        edge,
-        pltpu.roll(jnp.where(z0, edge_up, edge), 127, 1),
+
+
+def rotated(sources):
+    return [
+        pltpu.roll(source, turn, 1) if turn else source
+        for source, turn in zip(sources, (9, 8, 7, 1, 0, 127, 121, 120, 119))
+    ]
+
+
+def side_by_side(first, second):
+    return jnp.concatenate(
+        [jnp.concatenate([one, two], axis=1) for one, two in zip(first, second)], axis=0
     )
-    return middle, edges
-
-
-def second_stage(parts, masks, store):
-    _, _, y0, y7, _ = masks
-    middle, edges = parts
-    for c in range(3):
-        store(c, pltpu.roll(jnp.where(y7, edges[c], middle[c]), 8, 1))
-        store(3 + c, middle[c])
-        store(6 + c, pltpu.roll(jnp.where(y0, edges[c], middle[c]), 120, 1))
-
-
-def halo_stage(raw, masks):
-    _, _, y0, _, _ = masks
-    edge = pltpu.roll(jnp.where(y0, raw(1, 0), raw(-1, 0)), ROLLS[SWAP], 1)
-    edge_up = pltpu.roll(jnp.where(y0, raw(1, 1), raw(-1, 1)), ROLLS[SWAP_UP], 1)
-    edge_down = pltpu.roll(jnp.where(y0, raw(1, -1), raw(-1, -1)), ROLLS[SWAP_DOWN], 1)
-    up = pltpu.roll(raw(0, 1), ROLLS[UP], 1)
-    down = pltpu.roll(raw(0, -1), ROLLS[DOWN], 1)
-    return raw(0, 0), edge, edge_up, edge_down, up, down
-
-
-def halo_second(parts, masks):
-    z0, z7, _, _, _ = masks
-    centre, edge, edge_up, edge_down, up, down = parts
-    middle = (
-        pltpu.roll(jnp.where(z7, down, centre), 1, 1),
-        centre,
-        pltpu.roll(jnp.where(z0, up, centre), 127, 1),
-    )
-    edges = (
-        pltpu.roll(jnp.where(z7, edge_down, edge), 1, 1),
-        edge,
-        pltpu.roll(jnp.where(z0, edge_up, edge), 127, 1),
-    )
-    return middle, edges
+
+
+def halo_take(raw):
+    def take(kind, dy, dz):
+        piece = raw(dy, dz)
+        return pltpu.roll(piece, ROLLS[kind], 1) if ROLLS[kind] else piece
+
+    return take
 
 
 def columns(j):
@@ -140,7 +126,7 @@
 
 def inner_kernel(
     nb_ref, features_ref, occ_ref, gain_ref, shift_ref, weight_ref, edge_ref, middle_ref, wide,
-    acts, stack, ybuf, nb, sem,
+    acts, ybuf, nb, sem,
 ):
     copy = pltpu.make_async_copy(nb_ref, nb, sem)
     copy.start()
@@ -169,10 +155,10 @@
     rotate(BRK - 1)
     copy.wait()
 
-    def product(i, half):
+    def product(i, half, first, second):
         lanes = slice(2 * half * LANES, 2 * (half + 1) * LANES)
         ybuf[i % 2, :, lanes] = jnp.dot(
-            wide[...], stack[i % 2, :, lanes], preferred_element_type=F32
+            wide[...], side_by_side(first, second), preferred_element_type=F32
         )
 
     def finish(i, half):
@@ -192,36 +178,27 @@
             else:
                 middle_ref[i, :, columns(j - 1)] = total.astype(BF)
 
-    waiting = None
-    for i in range(BRK + 1):
-        if i < BRK:
-            slots = {
-                (dy, dz): i if (dy, dz) == (0, 0) else slot(nb, i, 0, dy, dz)
-                for dy in (-1, 0, 1)
-                for dz in (-1, 0, 1)
-            }
+    for i in range(BRK):
+        slots = {
+            (dy, dz): i if (dy, dz) == (0, 0) else slot(nb, i, 0, dy, dz)
+            for dy in (-1, 0, 1)
+            for dz in (-1, 0, 1)
+        }
+        pieces = []
         for j in range(4):
-            parts = None
-            if i < BRK:
-                parts = first_stage(
-                    lambda kind, dy, dz: acts[kind, slots[dy, dz], :, columns(j)], masks
+            pieces.append(
+                rotated(
+                    merged(lambda kind, dy, dz: acts[kind, slots[dy, dz], :, columns(j)], masks)
                 )
-            if waiting is not None:
-                oi, oj, old = waiting
-
-                def store(tap, piece):
-                    stack[oi % 2, tap * CH : (tap + 1) * CH, columns(oj)] = piece
-
-                second_stage(old, masks, store)
-            waiting = (i, j, parts) if parts is not None else None
-            if i < BRK and j == 3:
-                product(i, 0)
-            if i > 0 and j == 1:
-                product(i - 1, 1)
+            )
+            if j % 2 == 1:
+                product(i, j // 2, *pieces[-2:])
+            if i > 0 and j == 0:
+                finish(i - 1, 0)
             if i > 0 and j == 2:
-                finish(i - 1, 0)
-            if i > 0 and j == 3:
                 finish(i - 1, 1)
+    finish(BRK - 1, 0)
+    finish(BRK - 1, 1)
 
 
 def sorted_voxels(rows, sort_ref, picked, low):
@@ -254,7 +231,7 @@
     nb_ref, map_ref, edge_ref, middle_ref, chip_ref, far_ref, occ_ref, wide, stride_ref, bias_ref,
     sort_ref, entry_ref, place_ref,
     ends_ref, rows_ref, placing_ref, wide2, leave_ref,
-    halo, stack, picked, placing, mask, faces, leaving_ends, nb, map_, order, sems,
+    halo, picked, mask, faces, leaving_ends, nb, map_, order, sems,
 ):
     copies = [
         pltpu.make_async_copy(nb_ref, nb, sems.at[0]),
@@ -266,7 +243,7 @@
     device = lax.axis_index("bricks") * groups + lax.axis_index("grp")
     odd = lax.rem(device, 2)
     masks = lane_masks()
-    low = masks[4]
+    low = masks[2]
     low32 = lax.broadcasted_iota(jnp.int32, (CH, LANES), 1) < 64
     for i in range(BRK):
         halo[odd, i] = chip_ref[i]
@@ -301,10 +278,10 @@
 
         return raw
 
-    def product(pair):
+    def product(pair, one, two):
         lanes = slice(2 * pair * LANES, 2 * (pair + 1) * LANES)
         ends = jnp.concatenate([wide[:CH], wide[2 * CH :]], axis=0)
-        faces[:, lanes] = jnp.dot(ends, stack[:, lanes], preferred_element_type=F32)
+        faces[:, lanes] = jnp.dot(ends, side_by_side(one, two), preferred_element_type=F32)
 
     def finish(k):
         i = brick[k]
@@ -321,30 +298,22 @@
         if k >= HALF:
             rows_ref[k - HALF, :, : 2 * LANES] = middle_ref[i]
 
-    def place(k, target):
-        which = map_[0, brick[k]] & 7
-        part = slice(k % HALF * CH, (k % HALF + 1) * CH)
-        target[part, :] = entry_ref[...] * place_ref[which].astype(BF)
+    def place(k):
+        return entry_ref[...] * place_ref[map_[0, brick[k]] & 7].astype(BF)
 
     for k in range(HALF):
-        place(k, placing)
-        place(HALF + k, placing_ref)
-    first, second, result = None, None, None
-    for k in range(BRK + 2):
-        now = halo_stage(raw_of(brick[k]), masks) if k < BRK else None
-        later = halo_second(first, masks) if first is not None else None
-        if second is not None:
-            spot = k - 2
-
-            def store(tap, piece):
-                stack[tap * CH : (tap + 1) * CH, columns(spot)] = piece
-
-            second_stage(second, masks, store)
+        placing_ref[k * CH : (k + 1) * CH, :] = place(HALF + k)
+    before, result, pieces = None, None, []
+    for k in range(BRK + 1):
+        now = merged(halo_take(raw_of(brick[k])), masks) if k < BRK else None
+        if before is not None:
+            spot = k - 1
+            pieces.append(rotated(before))
             if spot == 2 or spot == 4 or spot == 6:
                 finish(spot - 2)
                 finish(spot - 1)
             if spot % 2 == 1:
-                product(spot // 2)
+                product(spot // 2, *pieces[-2:])
             if spot == 5:
                 rows = [
                     jnp.concatenate([middle_ref[brick[q]], leaving_ends[q]], axis=1)
@@ -355,9 +324,11 @@
                 result = octants(wide2, picked, bias)
             if spot == 7:
                 leave_ref[...] = jnp.dot(
-                    result, placing[...], preferred_element_type=F32
+                    result,
+                    jnp.concatenate([place(q) for q in range(HALF)], axis=0),
+                    preferred_element_type=F32,
                 ).astype(BF)
-        first, second = now, later
+        before = now
     finish(BRK - 2)
     finish(BRK - 1)
 
@@ -376,7 +347,7 @@
     ]
     for copy in copies:
         copy.start()
-    low = lane_masks()[4]
+    low = lane_masks()[2]
     sorted_voxels([rows_ref[k] for k in range(HALF)], sort_ref, picked, low)
     octant = octants(wide2, picked, column(bias_ref[...]))
     stay_ref[...] = jnp.dot(octant, placing_ref[...], preferred_element_type=F32).astype(BF)
@@ -451,7 +422,6 @@
         ),
         scratch_shapes=[
             pltpu.VMEM((len(ROLLS), BRK + 1, CH, VOX), BF),
-            pltpu.VMEM((2, TAPS * CH, VOX), BF),
             pltpu.VMEM((2, 3 * CH, VOX), F32),
             pltpu.SMEM((BRK, 26), jnp.int32),
             pltpu.SemaphoreType.DMA,
@@ -478,9 +448,7 @@
         ),
         scratch_shapes=[
             pltpu.VMEM((2, BRK + 1, CH, LANES), BF),
-            pltpu.VMEM((TAPS * CH, BRK * LANES), BF),
             pltpu.VMEM((2, 4 * CH, HALF * CH), BF),
-            pltpu.VMEM((HALF * CH, VOX), BF),
             pltpu.VMEM((BRK, 1, LANES), F32),
             pltpu.VMEM((2 * CH, BRK * LANES), F32),
             pltpu.VMEM((HALF, CH, 2 * LANES), BF),

time: 20.9 us -> 20 us (0.957)
  Pallas kernels: 8.12 us -> 7.22 us
    pallas_call x1, Pallas kernels: 3.71 us -> 2.93 us  [shards(): pl.pallas_call(inner_kernel, in_specs=[vmem] * 6, out_specs=[vmem] * 3, o...]
  transfers between devices with their start and end apart: 3 -> 3, of which waited for: 1 -> 1; matrix products, arithmetic and copies ran while one was open for 0% -> 0% of each run, Pallas kernels for 22% -> 19%
where the time goes in v5:
time: 20 us; the launch traced here: 19.9 us
  starting transfers between devices  10.8 us (54%)
  Pallas kernels  7.22 us (36%)
  between operations  0.73 us (4%)
  other arithmetic  0.67 us (3%)
  waiting for transfers between devices  0.43 us (2%)
    ppermute x1, starting transfers between devices, shards(): chip = lax.ppermute(face, 'grp', [(i, i ^ 1) for i in range(groups)])  6.92 us
    ppermute x1, starting transfers between devices, shards(): lax.ppermute(face, ('bricks', 'grp'), across + [(j, i) for i, j in across])  3.77 us
    pallas_call x1, Pallas kernels, shards(): pl.pallas_call(inner_kernel, in_specs=[vmem] * 6, out_specs=[vmem] * 3, o...  2.93 us
    pallas_call x1, Pallas kernels, shards(): pl.pallas_call(outer_kernel, in_specs=[vmem] * 13, out_specs=[vmem] * 5,...  2.12 us
    pallas_call x1, Pallas kernels, shards(): pl.pallas_call(faces_kernel, in_specs=[pl.BlockSpec(memory_space=pltpu.HB...  1.3 us
    pallas_call x1, Pallas kernels, shards(): pl.pallas_call(staying_kernel, in_specs=[vmem] * 7, out_specs=[pl.BlockSp...  0.87 us
    broadcast_in_dim x1, other arithmetic, shards(): return (fine, (stay + arrived)[None])  0.67 us
    ppermute x1, waiting for transfers between devices, shards(): arrived = lax.ppermute(leave, 'grp', [(i, i ^ 1) for i in range(groups)])  0.42 us
  transfers between devices with their start and end apart: 3, of which 1 were waited for; matrix products, arithmetic and copies ran while one was open for 0% of the time, Pallas kernels for 19%

profile of v5, /device:TPU:7, one launch (start us, length us, event | category | flops | bytes accessed | tf_op | source)
XLA Modules:
  0.0 19.9 jit_solution(5501870596160931285)
XLA Ops:
  0.6 1.3 %faces.1 = (bf16[8,64,128]{2,1,0:T(8,128)(2,1)S(1)}, bf16[8,64,512]{2,1,0:T(8,128)(2,1)S(1)}, s32[8,512]{1,0:T(8,128)S(1)}, f32[1,64]{1,0:T(1,128)S(1)}, f32[1,6...) custom-call(bf16[8,64,512]{2,1,0:T(8,128)(2,1)} %refs_0_.1, ...), custom_call_target="tpu_custom_call" | custom-call | tf_op jit(solution)/shard_map/faces/pallas_call | solution.py:398
  1.9 3.8 %collective-permute-start.1 = (bf16[8,64,128]{2,1,0:T(8,128)(2,1)S(1)}, bf16[8,64,128]{2,1,0:T(8,128)(2,1)S(1)}, u32[]{:S(2)}, u32[]{:S(2)}) collective-permute-start(bf16[8,64,128]{2,1,0:T(8,128)(2,1)S(1)} %get-tuple-element.30), channel_id=1, source_target_pairs={{1,2},{3,4},{5,6},{7,8},{9,10},{11,12},{13,14},{15,16},{17,18},{19... | collective-permute-start | bytes 393224 | tf_op jit(solution)/shard_map/ppermute | solution.py:412
  5.7 6.9 %collective-permute-start = (bf16[8,64,128]{2,1,0:T(8,128)(2,1)S(1)}, bf16[8,64,128]{2,1,0:T(8,128)(2,1)S(1)}, u32[]{:S(2)}, u32[]{:S(2)}) collective-permute-start(bf16[8,64,128]{2,1,0:T(8,128)(2,1)S(1)} %get-tuple-element.30), channel_id=1, source_target_pairs={{0,1},{1,0},{2,3},{3,2},{4,5},{5,4},{6,7},{7,6},{8,9},{9,8},{10,11... | collective-permute-start | bytes 393224 | tf_op jit(solution)/shard_map/ppermute | solution.py:410
  12.6 0.0 copy-start
  12.6 0.0 copy-start.1
  12.6 0.0 copy-start.2
  12.6 0.0 copy-start.3
  12.6 2.9 %inner.1 = (f32[8,64,256]{2,1,0:T(8,128)S(1)}, bf16[8,64,256]{2,1,0:T(8,128)(2,1)S(1)}, bf16[192,576]{1,0:T(8,128)(2,1)S(1)}) custom-call(s32[8,26]{1,0:T(8,128)S(1)} %get-tuple-element.21.nb_ref, bf16[8,64,512]{2,1,0:T(8,128)(2,1)S(1)} %get-tuple-element.23.features_ref, s32[8,512]{1,0:T(8,128)S(1)} %get-tuple-element.24.occ_ref, ...), custom_call_target="tpu_custom_call" | custom-call | flops 905969664 | bytes 2097152 | tf_op jit(solution)/shard_map/inner/pallas_call | solution.py:414
  15.6 0.0 collective-permute-done.1.far_ref
  15.6 0.0 collective-permute-done.chip_ref
  15.6 0.0 copy-done
  15.6 0.0 copy-done.1
  15.6 0.0 copy-done.2
  15.6 0.0 copy-done.3
  15.6 2.1 %outer.1 = (bf16[8,64,256]{2,1,0:T(8,128)(2,1)S(1)}, bf16[4,64,512]{2,1,0:T(8,128)(2,1)S(1)}, bf16[256,512]{1,0:T(8,128)(2,1)S(1)}, bf16[2,128,256]{2,1,0:T(8,128)(2,1)S(1)}, bf16[128,512]{1,0:T(8,128)(2,1)S(1)}) custom-call(s32[8,26]{1,0:T(8,128)S(1)} %get-tuple-element.21.nb_ref, s32[1,8]{1,0:T(1,128)S(1)} %get-tuple-element.22.map_ref, ...), custom_call_target="tpu_custom_call" | custom-call | tf_op jit(solution)/shard_map/outer/pallas_call | solution.py:438
  17.8 0.1 collective-permute-start.2
  17.9 0.9 %staying.1 = (bf16[8,64,512]{2,1,0:T(8,128)(2,1)}, bf16[128,512]{1,0:T(8,128)(2,1)S(1)}) custom-call(bf16[8,64,256]{2,1,0:T(8,128)(2,1)S(1)} %get-tuple-element.33.ends_ref, bf16[8,64,256]{2,1,0:T(8,128)(2,1)S(1)} %get-tuple-element.29.middle_ref, bf16[4,64,512]{2,1,0:T(8,128)(2,1)S(1)} %get-tuple-element.34.rows_ref, ...), custom_call_target="tpu_custom_call" | custom-call | flops 268435456 | bytes 2097152 | tf_op jit(solution)/shard_map/staying/pallas_call | solution.py:478
  18.8 0.4 %collective-permute-done.2 = bf16[128,512]{1,0:T(8,128)(2,1)S(1)} collective-permute-done((bf16[128,512]{1,0:T(8,128)(2,1)S(1)}, bf16[128,512]{1,0:T(8,128)(2,1)S(1)}, u32[]{:S(2)}, u32[]{:S(2)}) %collective-permute-start.2) | collective-permute-done | bytes 131104 | tf_op jit(solution)/shard_map/ppermute | solution.py:477
  19.2 0.7 %add_bitcast_fusion = bf16[1,128,512]{2,1,0:T(8,128)(2,1)} fusion(bf16[128,512]{1,0:T(8,128)(2,1)S(1)} %get-tuple-element.38, bf16[128,512]{1,0:T(8,128)(2,1)S(1)} %collective-permute-done.2), kind=kLoop, calls=%fused_computation | loop fusion | flops 65536 | bytes 393216 | tf_op jit(solution)/shard_map/broadcast_in_dim | solution.py:493
Async XLA Ops:
  1.9 13.6 %collective-permute-start.1 = (bf16[8,64,128]{2,1,0:T(8,128)(2,1)S(1)}, bf16[8,64,128]{2,1,0:T(8,128)(2,1)S(1)}, u32[]{:S(2)}, u32[]{:S(2)}) collective-permute-start(bf16[8,64,128]{2,1,0:T(8,128)(2,1)S(1)} %get-tuple-element.30), channel_id=1, source_target_pairs={{1,2},{3,4},{5,6},{7,8},{9,10},{11,12},{13,14},{15,16},{17,18},{19... | collective-permute-start | bytes 393224 | tf_op jit(solution)/shard_map/ppermute | solution.py:412
  5.7 9.9 %collective-permute-start = (bf16[8,64,128]{2,1,0:T(8,128)(2,1)S(1)}, bf16[8,64,128]{2,1,0:T(8,128)(2,1)S(1)}, u32[]{:S(2)}, u32[]{:S(2)}) collective-permute-start(bf16[8,64,128]{2,1,0:T(8,128)(2,1)S(1)} %get-tuple-element.30), channel_id=1, source_target_pairs={{0,1},{1,0},{2,3},{3,2},{4,5},{5,4},{6,7},{7,6},{8,9},{9,8},{10,11... | collective-permute-start | bytes 393224 | tf_op jit(solution)/shard_map/ppermute | solution.py:410
  12.6 3.0 %copy-start = (bf16[2,512,512]{2,1,0:T(8,128)(2,1)S(1)}, bf16[2,512,512]{2,1,0:T(8,128)(2,1)}, u32[]{:S(2)}) copy-start(bf16[2,512,512]{2,1,0:T(8,128)(2,1)} %constant.6.clone.sort_ref) | copy-start | bytes 3145732
  12.6 3.0 %copy-start.1 = (bf16[8,64,128]{2,1,0:T(8,128)(2,1)S(1)}, bf16[8,64,128]{2,1,0:T(8,128)(2,1)}, u32[]{:S(2)}) copy-start(bf16[8,64,128]{2,1,0:T(8,128)(2,1)} %stride_ref.1) | copy-start | bytes 393220
  12.6 3.0 %copy-start.2 = (bf16[64,512]{1,0:T(8,128)(2,1)S(1)}, bf16[64,512]{1,0:T(8,128)(2,1)}, u32[]{:S(2)}) copy-start(bf16[64,512]{1,0:T(8,128)(2,1)} %constant.7.clone.entry_ref) | copy-start | bytes 196612
  12.6 3.0 %copy-start.3 = (f32[8,1,512]{2,1,0:T(1,128)S(1)}, f32[8,1,512]{2,1,0:T(1,128)}, u32[]{:S(2)}) copy-start(f32[8,1,512]{2,1,0:T(1,128)} %constant.8.clone.place_ref) | copy-start | bytes 49156
  17.8 1.4 %collective-permute-start.2 = (bf16[128,512]{1,0:T(8,128)(2,1)S(1)}, bf16[128,512]{1,0:T(8,128)(2,1)S(1)}, u32[]{:S(2)}, u32[]{:S(2)}) collective-permute-start(bf16[128,512]{1,0:T(8,128)(2,1)S(1)} %get-tuple-element.39), channel_id=1, source_target_pairs={{0,1},{1,0},{2,3},{3,2},{4,5},{5,4},{6,7},{7,6},{8,9},{9,8},{10,11... | collective-permute-start | bytes 393224 | tf_op jit(solution)/shard_map/ppermute | solution.py:477

commit v6 on v5

--- a/solution.py
+++ b/solution.py
@@ -33,8 +33,11 @@
     return jnp.sum(jnp.where(on, wide, 0.0), axis=1, keepdims=True)
 
 
-def activate(x, occupied, gain):
-    scale = lax.rsqrt(jnp.mean(x * x, axis=0, keepdims=True) + EPS)
+def scale_of(x):
+    return lax.rsqrt(jnp.mean(x * x, axis=0, keepdims=True) + EPS)
+
+
+def activate(x, scale, occupied, gain):
     normed = x * scale * gain
     return (normed * jax.nn.sigmoid(normed) * occupied).astype(BF)
 
@@ -82,10 +85,8 @@
     ]
 
 
-def side_by_side(first, second):
-    return jnp.concatenate(
-        [jnp.concatenate([one, two], axis=1) for one, two in zip(first, second)], axis=0
-    )
+def side_by_side(*parts):
+    return jnp.concatenate([jnp.concatenate(row, axis=1) for row in zip(*parts)], axis=0)
 
 
 def halo_take(raw):
@@ -119,7 +120,7 @@
         x = jnp.where(low, first.astype(F32), last.astype(F32))
         row = slice(i, i + 1)
         occupied = jnp.where(low[:1], occ_ref[row, columns(0)], occ_ref[row, columns(3)])
-        face_ref[i] = activate(x, occupied.astype(F32), gain)
+        face_ref[i] = activate(x, scale_of(x), occupied.astype(F32), gain)
     for copy in copies[3:]:
         copy.wait()
 
@@ -137,17 +138,30 @@
     for kind in range(len(ROLLS)):
         acts[kind, BRK] = jnp.zeros((CH, VOX), BF)
 
+    lane = lax.broadcasted_iota(jnp.int32, (LANES, 2 * LANES), 1)
+    turn = jnp.where(lane < LANES, ROLLS[SWAP_UP], ROLLS[SWAP_DOWN])
+    origin = lax.broadcasted_iota(jnp.int32, (LANES, 2 * LANES), 0)
+    turns = (origin == ((lane - turn) & (LANES - 1))).astype(F32).astype(BF)
+
     def rotate(i):
         for j in range(4):
             piece = acts[PLAIN, i, :, columns(j)]
-            for kind in range(1, len(ROLLS)):
+            for kind in (SWAP, UP, DOWN):
                 acts[kind, i, :, columns(j)] = pltpu.roll(piece, ROLLS[kind], 1)
-
+        rows = jnp.concatenate([acts[PLAIN, i, :, columns(j)] for j in range(4)], axis=0)
+        both = jnp.dot(rows, turns, preferred_element_type=F32).astype(BF)
+        for j in range(4):
+            for k, kind in enumerate((SWAP_UP, SWAP_DOWN)):
+                acts[kind, i, :, columns(j)] = both[j * CH : (j + 1) * CH, columns(k)]
+
+    scale = scale_of(features_ref[0].astype(F32))
     for i in range(BRK):
+        upcoming = scale_of(features_ref[i + 1].astype(F32)) if i + 1 < BRK else None
         occupied = occ_ref[i : i + 1, :].astype(F32)
-        acts[PLAIN, i] = activate(features_ref[i].astype(F32), occupied, gain)
+        acts[PLAIN, i] = activate(features_ref[i].astype(F32), scale, occupied, gain)
         if i > 0:
             rotate(i - 1)
+        scale = upcoming
     for a in range(3):
         wide[a * CH : (a + 1) * CH, :] = (
             weight_ref[TAPS * a : TAPS * (a + 1)].reshape(TAPS * CH, CH).T
@@ -278,10 +292,10 @@
 
         return raw
 
-    def product(pair, one, two):
-        lanes = slice(2 * pair * LANES, 2 * (pair + 1) * LANES)
+    def product(half, pieces):
+        lanes = slice(HALF * half * LANES, HALF * (half + 1) * LANES)
         ends = jnp.concatenate([wide[:CH], wide[2 * CH :]], axis=0)
-        faces[:, lanes] = jnp.dot(ends, side_by_side(one, two), preferred_element_type=F32)
+        faces[:, lanes] = jnp.dot(ends, side_by_side(*pieces), preferred_element_type=F32)
 
     def finish(k):
         i = brick[k]
@@ -309,11 +323,11 @@
         if before is not None:
             spot = k - 1
             pieces.append(rotated(before))
-            if spot == 2 or spot == 4 or spot == 6:
-                finish(spot - 2)
-                finish(spot - 1)
-            if spot % 2 == 1:
-                product(spot // 2, *pieces[-2:])
+            if spot == 4:
+                for q in range(HALF):
+                    finish(q)
+            if spot % HALF == HALF - 1:
+                product(spot // HALF, pieces[-HALF:])
             if spot == 5:
                 rows = [
                     jnp.concatenate([middle_ref[brick[q]], leaving_ends[q]], axis=1)
@@ -329,8 +343,8 @@
                     preferred_element_type=F32,
                 ).astype(BF)
         before = now
-    finish(BRK - 2)
-    finish(BRK - 1)
+    for q in range(HALF, BRK):
+        finish(q)
 
 
 def staying_kernel(

time: 20 us -> 19.9 us (level)
  no operation moved by 1% of the time
where the time goes in v6:
time: 19.9 us; the launch traced here: 19.8 us
  starting transfers between devices  10.8 us (54%)
  Pallas kernels  7.14 us (36%)
  between operations  0.73 us (4%)
  other arithmetic  0.67 us (3%)
  waiting for transfers between devices  0.44 us (2%)
    ppermute x1, starting transfers between devices, shards(): chip = lax.ppermute(face, 'grp', [(i, i ^ 1) for i in range(groups)])  6.92 us
    ppermute x1, starting transfers between devices, shards(): lax.ppermute(face, ('bricks', 'grp'), across + [(j, i) for i, j in across])  3.77 us
    pallas_call x1, Pallas kernels, shards(): pl.pallas_call(inner_kernel, in_specs=[vmem] * 6, out_specs=[vmem] * 3, o...  2.88 us
    pallas_call x1, Pallas kernels, shards(): pl.pallas_call(outer_kernel, in_specs=[vmem] * 13, out_specs=[vmem] * 5,...  2.1 us
    pallas_call x1, Pallas kernels, shards(): pl.pallas_call(faces_kernel, in_specs=[pl.BlockSpec(memory_space=pltpu.HB...  1.3 us
    pallas_call x1, Pallas kernels, shards(): pl.pallas_call(staying_kernel, in_specs=[vmem] * 7, out_specs=[pl.BlockSp...  0.86 us
    broadcast_in_dim x1, other arithmetic, shards(): return (fine, (stay + arrived)[None])  0.67 us
    ppermute x1, waiting for transfers between devices, shards(): arrived = lax.ppermute(leave, 'grp', [(i, i ^ 1) for i in range(groups)])  0.43 us
  transfers between devices with their start and end apart: 3, of which 1 were waited for; matrix products, arithmetic and copies ran while one was open for 0% of the time, Pallas kernels for 19%

profile of v6, /device:TPU:7, one launch (start us, length us, event | category | flops | bytes accessed | tf_op | source)
XLA Modules:
  0.0 19.8 jit_solution(2294402625169011234)
XLA Ops:
  0.6 1.3 %faces.1 = (bf16[8,64,128]{2,1,0:T(8,128)(2,1)S(1)}, bf16[8,64,512]{2,1,0:T(8,128)(2,1)S(1)}, s32[8,512]{1,0:T(8,128)S(1)}, f32[1,64]{1,0:T(1,128)S(1)}, f32[1,6...) custom-call(bf16[8,64,512]{2,1,0:T(8,128)(2,1)} %refs_0_.1, ...), custom_call_target="tpu_custom_call" | custom-call | tf_op jit(solution)/shard_map/faces/pallas_call | solution.py:412
  1.9 3.8 %collective-permute-start.1 = (bf16[8,64,128]{2,1,0:T(8,128)(2,1)S(1)}, bf16[8,64,128]{2,1,0:T(8,128)(2,1)S(1)}, u32[]{:S(2)}, u32[]{:S(2)}) collective-permute-start(bf16[8,64,128]{2,1,0:T(8,128)(2,1)S(1)} %get-tuple-element.30), channel_id=1, source_target_pairs={{1,2},{3,4},{5,6},{7,8},{9,10},{11,12},{13,14},{15,16},{17,18},{19... | collective-permute-start | bytes 393224 | tf_op jit(solution)/shard_map/ppermute | solution.py:426
  5.7 6.9 %collective-permute-start = (bf16[8,64,128]{2,1,0:T(8,128)(2,1)S(1)}, bf16[8,64,128]{2,1,0:T(8,128)(2,1)S(1)}, u32[]{:S(2)}, u32[]{:S(2)}) collective-permute-start(bf16[8,64,128]{2,1,0:T(8,128)(2,1)S(1)} %get-tuple-element.30), channel_id=1, source_target_pairs={{0,1},{1,0},{2,3},{3,2},{4,5},{5,4},{6,7},{7,6},{8,9},{9,8},{10,11... | collective-permute-start | bytes 393224 | tf_op jit(solution)/shard_map/ppermute | solution.py:424
  12.6 0.0 copy-start
  12.6 0.0 copy-start.1
  12.6 0.0 copy-start.2
  12.6 0.0 copy-start.3
  12.6 2.9 %inner.1 = (f32[8,64,256]{2,1,0:T(8,128)S(1)}, bf16[8,64,256]{2,1,0:T(8,128)(2,1)S(1)}, bf16[192,576]{1,0:T(8,128)(2,1)S(1)}) custom-call(s32[8,26]{1,0:T(8,128)S(1)} %get-tuple-element.21.nb_ref, bf16[8,64,512]{2,1,0:T(8,128)(2,1)S(1)} %get-tuple-element.23.features_ref, s32[8,512]{1,0:T(8,128)S(1)} %get-tuple-element.24.occ_ref, ...), custom_call_target="tpu_custom_call" | custom-call | flops 905969664 | bytes 2097152 | tf_op jit(solution)/shard_map/inner/pallas_call | solution.py:428
  15.5 0.0 collective-permute-done.1.far_ref
  15.5 0.0 collective-permute-done.chip_ref
  15.5 0.0 copy-done
  15.6 0.0 copy-done.1
  15.6 0.0 copy-done.2
  15.6 0.0 copy-done.3
  15.6 2.1 %outer.1 = (bf16[8,64,256]{2,1,0:T(8,128)(2,1)S(1)}, bf16[4,64,512]{2,1,0:T(8,128)(2,1)S(1)}, bf16[256,512]{1,0:T(8,128)(2,1)S(1)}, bf16[2,128,256]{2,1,0:T(8,128)(2,1)S(1)}, bf16[128,512]{1,0:T(8,128)(2,1)S(1)}) custom-call(s32[8,26]{1,0:T(8,128)S(1)} %get-tuple-element.21.nb_ref, s32[1,8]{1,0:T(1,128)S(1)} %get-tuple-element.22.map_ref, ...), custom_call_target="tpu_custom_call" | custom-call | tf_op jit(solution)/shard_map/outer/pallas_call | solution.py:452
  17.7 0.1 collective-permute-start.2
  17.8 0.9 %staying.1 = (bf16[8,64,512]{2,1,0:T(8,128)(2,1)}, bf16[128,512]{1,0:T(8,128)(2,1)S(1)}) custom-call(bf16[8,64,256]{2,1,0:T(8,128)(2,1)S(1)} %get-tuple-element.33.ends_ref, bf16[8,64,256]{2,1,0:T(8,128)(2,1)S(1)} %get-tuple-element.29.middle_ref, bf16[4,64,512]{2,1,0:T(8,128)(2,1)S(1)} %get-tuple-element.34.rows_ref, ...), custom_call_target="tpu_custom_call" | custom-call | flops 268435456 | bytes 2097152 | tf_op jit(solution)/shard_map/staying/pallas_call | solution.py:492
  18.7 0.4 %collective-permute-done.2 = bf16[128,512]{1,0:T(8,128)(2,1)S(1)} collective-permute-done((bf16[128,512]{1,0:T(8,128)(2,1)S(1)}, bf16[128,512]{1,0:T(8,128)(2,1)S(1)}, u32[]{:S(2)}, u32[]{:S(2)}) %collective-permute-start.2) | collective-permute-done | bytes 131104 | tf_op jit(solution)/shard_map/ppermute | solution.py:491
  19.1 0.7 %add_bitcast_fusion = bf16[1,128,512]{2,1,0:T(8,128)(2,1)} fusion(bf16[128,512]{1,0:T(8,128)(2,1)S(1)} %get-tuple-element.38, bf16[128,512]{1,0:T(8,128)(2,1)S(1)} %collective-permute-done.2), kind=kLoop, calls=%fused_computation | loop fusion | flops 65536 | bytes 393216 | tf_op jit(solution)/shard_map/broadcast_in_dim | solution.py:507
Async XLA Ops:
  1.9 13.6 %collective-permute-start.1 = (bf16[8,64,128]{2,1,0:T(8,128)(2,1)S(1)}, bf16[8,64,128]{2,1,0:T(8,128)(2,1)S(1)}, u32[]{:S(2)}, u32[]{:S(2)}) collective-permute-start(bf16[8,64,128]{2,1,0:T(8,128)(2,1)S(1)} %get-tuple-element.30), channel_id=1, source_target_pairs={{1,2},{3,4},{5,6},{7,8},{9,10},{11,12},{13,14},{15,16},{17,18},{19... | collective-permute-start | bytes 393224 | tf_op jit(solution)/shard_map/ppermute | solution.py:426
  5.7 9.8 %collective-permute-start = (bf16[8,64,128]{2,1,0:T(8,128)(2,1)S(1)}, bf16[8,64,128]{2,1,0:T(8,128)(2,1)S(1)}, u32[]{:S(2)}, u32[]{:S(2)}) collective-permute-start(bf16[8,64,128]{2,1,0:T(8,128)(2,1)S(1)} %get-tuple-element.30), channel_id=1, source_target_pairs={{0,1},{1,0},{2,3},{3,2},{4,5},{5,4},{6,7},{7,6},{8,9},{9,8},{10,11... | collective-permute-start | bytes 393224 | tf_op jit(solution)/shard_map/ppermute | solution.py:424
  12.6 2.9 %copy-start = (bf16[2,512,512]{2,1,0:T(8,128)(2,1)S(1)}, bf16[2,512,512]{2,1,0:T(8,128)(2,1)}, u32[]{:S(2)}) copy-start(bf16[2,512,512]{2,1,0:T(8,128)(2,1)} %constant.6.clone.sort_ref) | copy-start | bytes 3145732
  12.6 2.9 %copy-start.1 = (bf16[8,64,128]{2,1,0:T(8,128)(2,1)S(1)}, bf16[8,64,128]{2,1,0:T(8,128)(2,1)}, u32[]{:S(2)}) copy-start(bf16[8,64,128]{2,1,0:T(8,128)(2,1)} %stride_ref.1) | copy-start | bytes 393220
  12.6 2.9 %copy-start.2 = (bf16[64,512]{1,0:T(8,128)(2,1)S(1)}, bf16[64,512]{1,0:T(8,128)(2,1)}, u32[]{:S(2)}) copy-start(bf16[64,512]{1,0:T(8,128)(2,1)} %constant.7.clone.entry_ref) | copy-start | bytes 196612
  12.6 2.9 %copy-start.3 = (f32[8,1,512]{2,1,0:T(1,128)S(1)}, f32[8,1,512]{2,1,0:T(1,128)}, u32[]{:S(2)}) copy-start(f32[8,1,512]{2,1,0:T(1,128)} %constant.8.clone.place_ref) | copy-start | bytes 49156
  17.7 1.4 %collective-permute-start.2 = (bf16[128,512]{1,0:T(8,128)(2,1)S(1)}, bf16[128,512]{1,0:T(8,128)(2,1)S(1)}, u32[]{:S(2)}, u32[]{:S(2)}) collective-permute-start(bf16[128,512]{1,0:T(8,128)(2,1)S(1)} %get-tuple-element.39), channel_id=1, source_target_pairs={{0,1},{1,0},{2,3},{3,2},{4,5},{5,4},{6,7},{7,6},{8,9},{9,8},{10,11... | collective-permute-start | bytes 393224 | tf_op jit(solution)/shard_map/ppermute | solution.py:491

commit v7 on v6

--- a/solution.py
+++ b/solution.py
@@ -315,8 +315,6 @@
     def place(k):
         return entry_ref[...] * place_ref[map_[0, brick[k]] & 7].astype(BF)
 
-    for k in range(HALF):
-        placing_ref[k * CH : (k + 1) * CH, :] = place(HALF + k)
     before, result, pieces = None, None, []
     for k in range(BRK + 1):
         now = merged(halo_take(raw_of(brick[k])), masks) if k < BRK else None
@@ -343,6 +341,8 @@
                     preferred_element_type=F32,
                 ).astype(BF)
         before = now
+    for k in range(HALF):
+        placing_ref[k * CH : (k + 1) * CH, :] = place(HALF + k)
     for q in range(HALF, BRK):
         finish(q)
 

time: 19.9 us -> 19.9 us (level)
  no operation moved by 1% of the time
where the time goes in v7:
time: 19.9 us; the launch traced here: 19.8 us
  starting transfers between devices  10.8 us (54%)
  Pallas kernels  7.14 us (36%)
  between operations  0.73 us (4%)
  other arithmetic  0.67 us (3%)
  waiting for transfers between devices  0.44 us (2%)
    ppermute x1, starting transfers between devices, shards(): chip = lax.ppermute(face, 'grp', [(i, i ^ 1) for i in range(groups)])  6.92 us
    ppermute x1, starting transfers between devices, shards(): lax.ppermute(face, ('bricks', 'grp'), across + [(j, i) for i, j in across])  3.77 us
    pallas_call x1, Pallas kernels, shards(): pl.pallas_call(inner_kernel, in_specs=[vmem] * 6, out_specs=[vmem] * 3, o...  2.88 us
    pallas_call x1, Pallas kernels, shards(): pl.pallas_call(outer_kernel, in_specs=[vmem] * 13, out_specs=[vmem] * 5,...  2.1 us
    pallas_call x1, Pallas kernels, shards(): pl.pallas_call(faces_kernel, in_specs=[pl.BlockSpec(memory_space=pltpu.HB...  1.3 us
    pallas_call x1, Pallas kernels, shards(): pl.pallas_call(staying_kernel, in_specs=[vmem] * 7, out_specs=[pl.BlockSp...  0.86 us
    broadcast_in_dim x1, other arithmetic, shards(): return (fine, (stay + arrived)[None])  0.67 us
    ppermute x1, waiting for transfers between devices, shards(): arrived = lax.ppermute(leave, 'grp', [(i, i ^ 1) for i in range(groups)])  0.43 us
  transfers between devices with their start and end apart: 3, of which 1 were waited for; matrix products, arithmetic and copies ran while one was open for 0% of the time, Pallas kernels for 19%

profile of v7, /device:TPU:7, one launch (start us, length us, event | category | flops | bytes accessed | tf_op | source)
XLA Modules:
  0.0 19.8 jit_solution(18439233456624073746)
XLA Ops:
  0.6 1.3 %faces.1 = (bf16[8,64,128]{2,1,0:T(8,128)(2,1)S(1)}, bf16[8,64,512]{2,1,0:T(8,128)(2,1)S(1)}, s32[8,512]{1,0:T(8,128)S(1)}, f32[1,64]{1,0:T(1,128)S(1)}, f32[1,6...) custom-call(bf16[8,64,512]{2,1,0:T(8,128)(2,1)} %refs_0_.1, ...), custom_call_target="tpu_custom_call" | custom-call | tf_op jit(solution)/shard_map/faces/pallas_call | solution.py:412
  1.9 3.8 %collective-permute-start.1 = (bf16[8,64,128]{2,1,0:T(8,128)(2,1)S(1)}, bf16[8,64,128]{2,1,0:T(8,128)(2,1)S(1)}, u32[]{:S(2)}, u32[]{:S(2)}) collective-permute-start(bf16[8,64,128]{2,1,0:T(8,128)(2,1)S(1)} %get-tuple-element.30), channel_id=1, source_target_pairs={{1,2},{3,4},{5,6},{7,8},{9,10},{11,12},{13,14},{15,16},{17,18},{19... | collective-permute-start | bytes 393224 | tf_op jit(solution)/shard_map/ppermute | solution.py:426
  5.7 6.9 %collective-permute-start = (bf16[8,64,128]{2,1,0:T(8,128)(2,1)S(1)}, bf16[8,64,128]{2,1,0:T(8,128)(2,1)S(1)}, u32[]{:S(2)}, u32[]{:S(2)}) collective-permute-start(bf16[8,64,128]{2,1,0:T(8,128)(2,1)S(1)} %get-tuple-element.30), channel_id=1, source_target_pairs={{0,1},{1,0},{2,3},{3,2},{4,5},{5,4},{6,7},{7,6},{8,9},{9,8},{10,11... | collective-permute-start | bytes 393224 | tf_op jit(solution)/shard_map/ppermute | solution.py:424
  12.6 0.0 copy-start
  12.6 0.0 copy-start.1
  12.6 0.0 copy-start.2
  12.6 0.0 copy-start.3
  12.6 2.9 %inner.1 = (f32[8,64,256]{2,1,0:T(8,128)S(1)}, bf16[8,64,256]{2,1,0:T(8,128)(2,1)S(1)}, bf16[192,576]{1,0:T(8,128)(2,1)S(1)}) custom-call(s32[8,26]{1,0:T(8,128)S(1)} %get-tuple-element.21.nb_ref, bf16[8,64,512]{2,1,0:T(8,128)(2,1)S(1)} %get-tuple-element.23.features_ref, s32[8,512]{1,0:T(8,128)S(1)} %get-tuple-element.24.occ_ref, ...), custom_call_target="tpu_custom_call" | custom-call | flops 905969664 | bytes 2097152 | tf_op jit(solution)/shard_map/inner/pallas_call | solution.py:428
  15.5 0.0 collective-permute-done.1.far_ref
  15.5 0.0 collective-permute-done.chip_ref
  15.5 0.0 copy-done
  15.6 0.0 copy-done.1
  15.6 0.0 copy-done.2
  15.6 0.0 copy-done.3
  15.6 2.1 %outer.1 = (bf16[8,64,256]{2,1,0:T(8,128)(2,1)S(1)}, bf16[4,64,512]{2,1,0:T(8,128)(2,1)S(1)}, bf16[256,512]{1,0:T(8,128)(2,1)S(1)}, bf16[2,128,256]{2,1,0:T(8,128)(2,1)S(1)}, bf16[128,512]{1,0:T(8,128)(2,1)S(1)}) custom-call(s32[8,26]{1,0:T(8,128)S(1)} %get-tuple-element.21.nb_ref, s32[1,8]{1,0:T(1,128)S(1)} %get-tuple-element.22.map_ref, ...), custom_call_target="tpu_custom_call" | custom-call | tf_op jit(solution)/shard_map/outer/pallas_call | solution.py:452
  17.7 0.1 collective-permute-start.2
  17.8 0.9 %staying.1 = (bf16[8,64,512]{2,1,0:T(8,128)(2,1)}, bf16[128,512]{1,0:T(8,128)(2,1)S(1)}) custom-call(bf16[8,64,256]{2,1,0:T(8,128)(2,1)S(1)} %get-tuple-element.33.ends_ref, bf16[8,64,256]{2,1,0:T(8,128)(2,1)S(1)} %get-tuple-element.29.middle_ref, bf16[4,64,512]{2,1,0:T(8,128)(2,1)S(1)} %get-tuple-element.34.rows_ref, ...), custom_call_target="tpu_custom_call" | custom-call | flops 268435456 | bytes 2097152 | tf_op jit(solution)/shard_map/staying/pallas_call | solution.py:492
  18.7 0.4 %collective-permute-done.2 = bf16[128,512]{1,0:T(8,128)(2,1)S(1)} collective-permute-done((bf16[128,512]{1,0:T(8,128)(2,1)S(1)}, bf16[128,512]{1,0:T(8,128)(2,1)S(1)}, u32[]{:S(2)}, u32[]{:S(2)}) %collective-permute-start.2) | collective-permute-done | bytes 131104 | tf_op jit(solution)/shard_map/ppermute | solution.py:491
  19.1 0.7 %add_bitcast_fusion = bf16[1,128,512]{2,1,0:T(8,128)(2,1)} fusion(bf16[128,512]{1,0:T(8,128)(2,1)S(1)} %get-tuple-element.38, bf16[128,512]{1,0:T(8,128)(2,1)S(1)} %collective-permute-done.2), kind=kLoop, calls=%fused_computation | loop fusion | flops 65536 | bytes 393216 | tf_op jit(solution)/shard_map/broadcast_in_dim | solution.py:507
Async XLA Ops:
  1.9 13.6 %collective-permute-start.1 = (bf16[8,64,128]{2,1,0:T(8,128)(2,1)S(1)}, bf16[8,64,128]{2,1,0:T(8,128)(2,1)S(1)}, u32[]{:S(2)}, u32[]{:S(2)}) collective-permute-start(bf16[8,64,128]{2,1,0:T(8,128)(2,1)S(1)} %get-tuple-element.30), channel_id=1, source_target_pairs={{1,2},{3,4},{5,6},{7,8},{9,10},{11,12},{13,14},{15,16},{17,18},{19... | collective-permute-start | bytes 393224 | tf_op jit(solution)/shard_map/ppermute | solution.py:426
  5.7 9.8 %collective-permute-start = (bf16[8,64,128]{2,1,0:T(8,128)(2,1)S(1)}, bf16[8,64,128]{2,1,0:T(8,128)(2,1)S(1)}, u32[]{:S(2)}, u32[]{:S(2)}) collective-permute-start(bf16[8,64,128]{2,1,0:T(8,128)(2,1)S(1)} %get-tuple-element.30), channel_id=1, source_target_pairs={{0,1},{1,0},{2,3},{3,2},{4,5},{5,4},{6,7},{7,6},{8,9},{9,8},{10,11... | collective-permute-start | bytes 393224 | tf_op jit(solution)/shard_map/ppermute | solution.py:424
  12.6 2.9 %copy-start = (bf16[2,512,512]{2,1,0:T(8,128)(2,1)S(1)}, bf16[2,512,512]{2,1,0:T(8,128)(2,1)}, u32[]{:S(2)}) copy-start(bf16[2,512,512]{2,1,0:T(8,128)(2,1)} %constant.6.clone.sort_ref) | copy-start | bytes 3145732
  12.6 2.9 %copy-start.1 = (bf16[8,64,128]{2,1,0:T(8,128)(2,1)S(1)}, bf16[8,64,128]{2,1,0:T(8,128)(2,1)}, u32[]{:S(2)}) copy-start(bf16[8,64,128]{2,1,0:T(8,128)(2,1)} %stride_ref.1) | copy-start | bytes 393220
  12.6 2.9 %copy-start.2 = (bf16[64,512]{1,0:T(8,128)(2,1)S(1)}, bf16[64,512]{1,0:T(8,128)(2,1)}, u32[]{:S(2)}) copy-start(bf16[64,512]{1,0:T(8,128)(2,1)} %constant.7.clone.entry_ref) | copy-start | bytes 196612
  12.6 2.9 %copy-start.3 = (f32[8,1,512]{2,1,0:T(1,128)S(1)}, f32[8,1,512]{2,1,0:T(1,128)}, u32[]{:S(2)}) copy-start(f32[8,1,512]{2,1,0:T(1,128)} %constant.8.clone.place_ref) | copy-start | bytes 49156
  17.7 1.4 %collective-permute-start.2 = (bf16[128,512]{1,0:T(8,128)(2,1)S(1)}, bf16[128,512]{1,0:T(8,128)(2,1)S(1)}, u32[]{:S(2)}, u32[]{:S(2)}) collective-permute-start(bf16[128,512]{1,0:T(8,128)(2,1)S(1)} %get-tuple-element.39), channel_id=1, source_target_pairs={{0,1},{1,0},{2,3},{3,2},{4,5},{5,4},{6,7},{7,6},{8,9},{9,8},{10,11... | collective-permute-start | bytes 393224 | tf_op jit(solution)/shard_map/ppermute | solution.py:491
